TPU v7x, 32 devices: a whole 2x2x4 slice. The times are simulated.
32 devices in a mesh: dp: 8 (over z, y), tensor: 4 (over x, core).
Axes of the slice: x: 2, y: 2, z: 4, core: 2. Of those that a mesh axis runs over, the one named last changes fastest.
Arguments:
- features: float32 [512, 49, 2048], P('dp', None, 'tensor'), may hold values from -6 to 6
- frame_clip: int32 [512], P('dp'), may hold values from -1 to 127, as said below
- reduce_first: float32 [2048, 512], P(None, 'tensor'), may hold values from -0.125 to 0.125
- gain_reduce: float32 [512], P('tensor'), may hold values from 0.5 to 1.5
- bias_reduce: float32 [512], P('tensor'), may hold values from -1.2 to 1.2
- motion_down: float32 [512, 32], P('tensor'), may hold values from -0.25 to 0.25
- motion_kernel: float32 [9, 32], replicated, may hold values from -3.5 to 3.5
- motion_up: float32 [32, 512], P(None, 'tensor'), may hold values from -3 to 3
- motion_bias: float32 [512], P('tensor'), may hold values from -4 to 4
- group_taps: float32 [4, 3, 128], P('tensor'), may hold values from -3 to 3
- group_spatial: float32 [4, 1152, 128], P('tensor'), may hold values from -0.1875 to 0.1875
- gain_groups: float32 [512], P('tensor'), may hold values from 0.5 to 1.5
- bias_groups: float32 [512], P('tensor'), may hold values from -1.2 to 1.2
- expand_first: float32 [512, 2048], P('tensor'), may hold values from -0.25 to 0.25
- gain_expand: float32 [2048], P('tensor'), may hold values from 0.5 to 1.5
- bias_expand: float32 [2048], P('tensor'), may hold values from -1.2 to 1.2
- reduce_second: float32 [2048, 512], P(None, 'tensor'), may hold values from -0.125 to 0.125
- gain_narrow: float32 [512], P('tensor'), may hold values from 0.5 to 1.5
- bias_narrow: float32 [512], P('tensor'), may hold values from -1.2 to 1.2
- spatial_second: float32 [4608, 512], P(None, 'tensor'), may hold values from -0.09375 to 0.09375
- gain_spatial: float32 [512], P('tensor'), may hold values from 0.5 to 1.5
- bias_spatial: float32 [512], P('tensor'), may hold values from -1.2 to 1.2
- expand_second: float32 [512, 2048], P('tensor'), may hold values from -0.25 to 0.25
- gain_output: float32 [2048], P('tensor'), may hold values from 0.5 to 1.5
- bias_output: float32 [2048], P('tensor'), may hold values from -1.2 to 1.2
- cotangent: float32 [512, 49, 2048], P('dp', None, 'tensor'), may hold values from -6 to 6
Outputs:
- output: float32 [512, 49, 2048], P('dp', None, 'tensor')
- grad_features: float32 [512, 49, 2048], P('dp', None, 'tensor')
- grad_reduce_first: float32 [2048, 512], P(None, 'tensor')
- grad_gain_reduce: float32 [512], P('tensor')
- grad_bias_reduce: float32 [512], P('tensor')
- grad_motion_down: float32 [512, 32], P('tensor')
- grad_motion_kernel: float32 [9, 32], replicated
- grad_motion_up: float32 [32, 512], P(None, 'tensor')
- grad_motion_bias: float32 [512], P('tensor')
- grad_group_taps: float32 [4, 3, 128], P('tensor')
- grad_group_spatial: float32 [4, 1152, 128], P('tensor')
- grad_gain_groups: float32 [512], P('tensor')
- grad_bias_groups: float32 [512], P('tensor')
- grad_expand_first: float32 [512, 2048], P('tensor')
- grad_gain_expand: float32 [2048], P('tensor')
- grad_bias_expand: float32 [2048], P('tensor')
- grad_reduce_second: float32 [2048, 512], P(None, 'tensor')
- grad_gain_narrow: float32 [512], P('tensor')
- grad_bias_narrow: float32 [512], P('tensor')
- grad_spatial_second: float32 [4608, 512], P(None, 'tensor')
- grad_gain_spatial: float32 [512], P('tensor')
- grad_bias_spatial: float32 [512], P('tensor')
- grad_expand_second: float32 [512, 2048], P('tensor')
- grad_gain_output: float32 [2048], P('tensor')
- grad_bias_output: float32 [2048], P('tensor')
Inputs may be any that keep to these rules, and one draw needn't show every extreme that they name: `frame_clip`: each device's 64 slots hold whole clips in consecutive slots, clip numbers differ between devices, every clip has 4 to 48 frames, every device's first clip has 48 frames, and -1 slots come after a device's last clip.
All inputs are finite; a program needn't handle non-finite values.
Results may differ from a plain program's by a relative error of at most 0.0095.
Values sent between devices are 32-bit elements; how exact they have to be, the bound alone decides.
A program may use at most 640 MiB of HBM per device.

v0:
```python
import jax
import jax.numpy as jnp
from jax import lax
from jax.sharding import PartitionSpec as P

SIDE = 7


HIGH = lax.Precision.HIGHEST
EPS = 1e-05


def shifted_2(value, axis, steps):
    count = lax.axis_size(axis)
    initial, last = (max(0, -steps), min(count, count - steps))
    return lax.ppermute(value, axis, [(source, source + steps) for source in range(initial, last)])


def dense(values, weight):
    flat = values.reshape(-1, values.shape[-1])
    return jnp.dot(flat, weight, precision=HIGH).reshape(values.shape[:-1] + (weight.shape[1],))


def back_dense(grad, weight):
    flat = grad.reshape(-1, grad.shape[-1])
    result = lax.dot_general(flat, weight, (((1,), (1,)), ((), ())), precision=HIGH)
    return result.reshape(grad.shape[:-1] + (weight.shape[0],))


def weight_grad(left, right):
    flat_left = left.reshape(-1, left.shape[-1])
    flat_right = right.reshape(-1, right.shape[-1])
    return lax.dot_general(flat_left, flat_right, (((0,), (0,)), ((), ())), precision=HIGH)


def frame_taps(values):
    frames, cells, chans = values.shape
    grid = values.reshape(frames, SIDE, SIDE, chans)
    padded = jnp.pad(grid, ((0, 0), (1, 1), (1, 1), (0, 0)))
    return [
        padded[:, row : row + SIDE, col : col + SIDE, :].reshape(frames, cells, chans)
        for row in range(3)
        for col in range(3)
    ]


def stack_taps(values):
    return jnp.concatenate(frame_taps(values), axis=-1)


def depthwise(values, kernel):
    pieces = frame_taps(values)
    total = pieces[0] * kernel[0]
    for index in range(1, 9):
        total = total + pieces[index] * kernel[index]
    return total


def next_frame(values):
    return jnp.concatenate([values[1:], jnp.zeros_like(values[:1])], axis=0)


def prev_frame(values):
    return jnp.concatenate([jnp.zeros_like(values[:1]), values[:-1]], axis=0)


def temporal(values, kernel, prev_same, next_same):
    return (
        kernel[0] * prev_frame(values) * prev_same
        + kernel[1] * values
        + kernel[2] * next_frame(values) * next_same
    )


def group_conv(values, kernel, weight, prev_same, next_same):
    return dense(stack_taps(temporal(values, kernel, prev_same, next_same)), weight)


def motion_pool(summed, kernel, next_same):
    shifted = next_frame(depthwise(summed, kernel))
    return jnp.mean(next_same * (shifted - summed), axis=1)


def motion_gate(pooled, up_weight, up_bias):
    return jax.nn.sigmoid(jnp.dot(pooled, up_weight, precision=HIGH) + up_bias)


def scale_shift(values, mean, var, gain, bias):
    return gain * (values - mean) * lax.rsqrt(var + EPS) + bias


def channels_all(values):
    return lax.all_gather(values, "tensor", axis=2, tiled=True)


def channels_part(values):
    return lax.psum_scatter(values, "tensor", scatter_dimension=2, tiled=True)


def batch_total(values):
    return lax.psum(values, "dp")


def norm_forward(values, mrow, count, gain, bias, total):
    mean = total(jnp.sum(values * mrow, axis=(0, 1))) / count
    centered = values - mean
    var = total(jnp.sum(mrow * centered * centered, axis=(0, 1))) / count
    normed, pull = jax.vjp(scale_shift, values, mean, var, gain, bias)

    def backward(grad):
        dvalues, dmean, dvar, dgain, dbias = pull(grad)
        dsecond = total(dvar) / count
        centered = values - mean
        local_mean = dmean - 2.0 * dsecond * jnp.sum(mrow * centered, axis=(0, 1))
        dfirst = total(local_mean) / count
        dvalues = dvalues + mrow * (2.0 * dsecond * centered + dfirst)
        return (dvalues, dgain, dbias)

    return (normed, backward)


def positive(values):
    return (values > 0).astype(jnp.float32)


def channel_layout(features, cotangent, weights, mrow, next_same, prev_same, count):
    (
        reduce_first,
        gain_reduce,
        bias_reduce,
        motion_down,
        motion_kernel,
        motion_up,
        motion_bias,
        group_taps,
        group_spatial,
        gain_groups,
        bias_groups,
        expand_first,
        gain_expand,
        bias_expand,
        reduce_second,
        gain_narrow,
        bias_narrow,
        spatial_second,
        gain_spatial,
        bias_spatial,
        expand_second,
        gain_output,
        bias_output,
    ) = weights
    group_count = lax.axis_size("tensor")
    widened = channels_all(features)
    first_norm, first_back = norm_forward(
        dense(widened, reduce_first), mrow, count, gain_reduce, bias_reduce, batch_total
    )
    first_act = jnp.maximum(first_norm, 0.0)
    motion_total = lax.psum(dense(first_act, motion_down), "tensor")
    pooled, pool_back = jax.vjp(
        lambda summed, kernel: motion_pool(summed, kernel, next_same), motion_total, motion_kernel
    )
    gate, gate_back = jax.vjp(motion_gate, pooled, motion_up, motion_bias)
    excited = first_act * gate[:, None, :]
    taps_weight = group_taps[0]
    spatial_weight = group_spatial[0]

    def group_step(values, kernel, weight):
        return group_conv(values, kernel, weight, prev_same, next_same)

    incoming = jnp.zeros_like(excited)
    grouped = group_step(excited, taps_weight, spatial_weight)
    for step in range(1, group_count):
        incoming = shifted_2(grouped, "tensor", 1)
        grouped = group_step(excited + incoming, taps_weight, spatial_weight)
    mixed_norm, mixed_back = norm_forward(
        grouped, mrow, count, gain_groups, bias_groups, batch_total
    )
    mixed_act = jnp.maximum(mixed_norm, 0.0)
    expanded = channels_part(dense(mixed_act, expand_first))
    out_norm, out_back = norm_forward(expanded, mrow, count, gain_expand, bias_expand, batch_total)
    block_pre = out_norm + features
    middle = jnp.maximum(block_pre, 0.0)
    wide_middle = channels_all(middle)
    narrow_norm, narrow_back = norm_forward(
        dense(wide_middle, reduce_second), mrow, count, gain_narrow, bias_narrow, batch_total
    )
    narrow_act = jnp.maximum(narrow_norm, 0.0)
    narrow_all = channels_all(narrow_act)
    stacked, stack_back = jax.vjp(stack_taps, narrow_all)
    conv_norm, conv_back = norm_forward(
        dense(stacked, spatial_second), mrow, count, gain_spatial, bias_spatial, batch_total
    )
    conv_act = jnp.maximum(conv_norm, 0.0)
    final_pre = channels_part(dense(conv_act, expand_second))
    final_norm, final_back = norm_forward(
        final_pre, mrow, count, gain_output, bias_output, batch_total
    )
    last_pre = final_norm + middle
    output = mrow * jnp.maximum(last_pre, 0.0)
    grad_last = cotangent * mrow * positive(last_pre)
    dfinal, g_gain_output, g_bias_output = final_back(grad_last)
    dfinal_all = channels_all(dfinal)
    g_expand_second = weight_grad(conv_act, dfinal_all)
    dconv_act = back_dense(dfinal_all, expand_second) * positive(conv_norm)
    dconv, g_gain_spatial, g_bias_spatial = conv_back(dconv_act)
    g_spatial_second = weight_grad(stacked, dconv)
    dnarrow_all = stack_back(back_dense(dconv, spatial_second))[0]
    dnarrow_act = channels_part(dnarrow_all) * positive(narrow_norm)
    dnarrow, g_gain_narrow, g_bias_narrow = narrow_back(dnarrow_act)
    g_reduce_second = weight_grad(wide_middle, dnarrow)
    dmiddle = grad_last + channels_part(back_dense(dnarrow, reduce_second))
    dblock = dmiddle * positive(block_pre)
    dexpanded, g_gain_expand, g_bias_expand = out_back(dblock)
    dexpanded_all = channels_all(dexpanded)
    g_expand_first = weight_grad(mixed_act, dexpanded_all)
    dmixed_act = back_dense(dexpanded_all, expand_first) * positive(mixed_norm)
    dgrouped, g_gain_groups, g_bias_groups = mixed_back(dmixed_act)
    unused, group_pull = jax.vjp(group_step, excited + incoming, taps_weight, spatial_weight)
    dinput, dtaps, dspatial = group_pull(dgrouped)
    for step in range(1, group_count):
        from_right = shifted_2(dinput, "tensor", -1)
        dinput, dtaps, dspatial = group_pull(dgrouped + from_right)
    dfirst_act = dinput * gate[:, None, :]
    dgate = jnp.sum(dinput * first_act, axis=1)
    dpooled_local, g_motion_up, g_motion_bias = gate_back(dgate)
    dpooled = lax.psum(dpooled_local, "tensor")
    dmotion_total, g_motion_kernel = pool_back(dpooled)
    g_motion_down = weight_grad(first_act, dmotion_total)
    dfirst_act = (dfirst_act + back_dense(dmotion_total, motion_down)) * positive(first_norm)
    dfirst, g_gain_reduce, g_bias_reduce = first_back(dfirst_act)
    g_reduce_first = weight_grad(widened, dfirst)
    grad_features = dblock + channels_part(back_dense(dfirst, reduce_first))
    grads = (
        g_reduce_first,
        g_gain_reduce,
        g_bias_reduce,
        g_motion_down,
        g_motion_kernel,
        g_motion_up,
        g_motion_bias,
        dtaps[None],
        dspatial[None],
        g_gain_groups,
        g_bias_groups,
        g_expand_first,
        g_gain_expand,
        g_bias_expand,
        g_reduce_second,
        g_gain_narrow,
        g_bias_narrow,
        g_spatial_second,
        g_gain_spatial,
        g_bias_spatial,
        g_expand_second,
        g_gain_output,
        g_bias_output,
    )
    return (output, grad_features, grads)


def local(
    features,
    frame_clip,
    reduce_first,
    gain_reduce,
    bias_reduce,
    motion_down,
    motion_kernel,
    motion_up,
    motion_bias,
    group_taps,
    group_spatial,
    gain_groups,
    bias_groups,
    expand_first,
    gain_expand,
    bias_expand,
    reduce_second,
    gain_narrow,
    bias_narrow,
    spatial_second,
    gain_spatial,
    bias_spatial,
    expand_second,
    gain_output,
    bias_output,
    cotangent,
):
    valid = (frame_clip >= 0).astype(jnp.float32)
    after = jnp.concatenate([frame_clip[1:], jnp.full((1,), -2, jnp.int32)])
    before = jnp.concatenate([jnp.full((1,), -2, jnp.int32), frame_clip[:-1]])
    next_same = ((frame_clip >= 0) & (after == frame_clip)).astype(jnp.float32)[:, None, None]
    prev_same = ((frame_clip >= 0) & (before == frame_clip)).astype(jnp.float32)[:, None, None]
    mrow = valid[:, None, None]
    count = batch_total(jnp.sum(valid) * (SIDE * SIDE))
    weights = (
        reduce_first,
        gain_reduce,
        bias_reduce,
        motion_down,
        motion_kernel,
        motion_up,
        motion_bias,
        group_taps,
        group_spatial,
        gain_groups,
        bias_groups,
        expand_first,
        gain_expand,
        bias_expand,
        reduce_second,
        gain_narrow,
        bias_narrow,
        spatial_second,
        gain_spatial,
        bias_spatial,
        expand_second,
        gain_output,
        bias_output,
    )
    output, grad_features, grads = channel_layout(
        features, cotangent, weights, mrow, next_same, prev_same, count
    )
    summed = lax.psum(
        (
            grads[0],
            grads[1],
            grads[2],
            grads[3],
            grads[4],
            grads[5],
            grads[6],
            grads[7],
            grads[8],
            grads[9],
            grads[10],
            grads[11],
            grads[12],
            grads[13],
            grads[14],
            grads[15],
            grads[16],
            grads[17],
            grads[18],
            grads[19],
            grads[20],
            grads[21],
            grads[22],
        ),
        "dp",
    )
    return (
        output,
        grad_features,
        summed[0],
        summed[1],
        summed[2],
        summed[3],
        summed[4],
        summed[5],
        summed[6],
        summed[7],
        summed[8],
        summed[9],
        summed[10],
        summed[11],
        summed[12],
        summed[13],
        summed[14],
        summed[15],
        summed[16],
        summed[17],
        summed[18],
        summed[19],
        summed[20],
        summed[21],
        summed[22],
    )


def solution(mesh):
    placed = (
        P("dp", None, "tensor"),
        P("dp"),
        P(None, "tensor"),
        P("tensor"),
        P("tensor"),
        P("tensor", None),
        P(),
        P(None, "tensor"),
        P("tensor"),
        P("tensor", None, None),
        P("tensor", None, None),
        P("tensor"),
        P("tensor"),
        P("tensor", None),
        P("tensor"),
        P("tensor"),
        P(None, "tensor"),
        P("tensor"),
        P("tensor"),
        P(None, "tensor"),
        P("tensor"),
        P("tensor"),
        P("tensor", None),
        P("tensor"),
        P("tensor"),
        P("dp", None, "tensor"),
    )
    return jax.shard_map(
        local,
        mesh=mesh,
        in_specs=placed,
        out_specs=(
            P("dp", None, "tensor"),
            P("dp", None, "tensor"),
            P(None, "tensor"),
            P("tensor"),
            P("tensor"),
            P("tensor", None),
            P(),
            P(None, "tensor"),
            P("tensor"),
            P("tensor", None, None),
            P("tensor", None, None),
            P("tensor"),
            P("tensor"),
            P("tensor", None),
            P("tensor"),
            P("tensor"),
            P(None, "tensor"),
            P("tensor"),
            P("tensor"),
            P(None, "tensor"),
            P("tensor"),
            P("tensor"),
            P("tensor", None),
            P("tensor"),
            P("tensor"),
        ),
        check_vma=False,
    )
```

profile of v0, /device:TPU:0, one launch (start us, length us, event | category | flops | bytes accessed | tf_op | source)
XLA Modules:
  0.0 3350.9 jit_solution(11498381054027532771)
XLA Ops:
  9.6 160.5 %all-gather.6.cloned.1.call-done = f32[64,49,2048]{2,0,1:T(8,128)} async-done(((f32[64,49,512]{2,0,1:T(8,128)}), f32[64,49,2048]{2,0,1:T(8,128)}) %all-gather.6.cloned.1.call-update) | async-done | bytes 25690128 | tf_op jit(solution)/shard_map/all_gather | solution.py:93
  170.1 24.2 multiply_reduce_fusion.28
  194.3 22.0 all-reduce.91
  244.4 32.3 all-reduce.96.cloned.1.call-done
  331.7 18.5 collective-permute-start.1
  373.3 19.3 collective-permute-start.2
  415.0 21.9 psum.354
  459.0 24.4 fusion.27
  483.5 200.6 %reduce-scatter.6.cloned.1.call-done = f32[64,49,512]{2,0,1:T(8,128)} async-done(((f32[64,49,2048]{2,0,1:T(8,128)}), f32[64,49,512]{2,0,1:T(8,128)}) %reduce-scatter.6.cloned.1.call-update) | async-done | bytes 6422544 | tf_op jit(solution)/shard_map/reduce_scatter | solution.py:97
  687.6 21.4 psum.356
  742.1 155.3 %all-gather.8.cloned.1.call-done = f32[64,49,2048]{2,0,1:T(8,128)} async-done(((f32[64,49,512]{2,0,1:T(8,128)}), f32[64,49,2048]{2,0,1:T(8,128)}) %all-gather.8.cloned.1.call-update) | async-done | bytes 25690128 | tf_op jit(solution)/shard_map/all_gather | solution.py:93
  897.5 24.2 multiply_reduce_fusion.26
  921.7 21.5 psum.358
  968.0 45.4 %all-gather.10.cloned.1.call-done = f32[64,49,512]{2,0,1:T(8,128)} async-done(((f32[64,49,128]{2,0,1:T(8,128)}), f32[64,49,512]{2,0,1:T(8,128)}) %all-gather.10.cloned.1.call-update) | async-done | bytes 6422544 | tf_op jit(solution)/shard_map/all_gather | solution.py:93
  1013.4 33.6 %pad_slice_fusion = (f32[64,7,7,512]{3,0,2,1:T(8,128)}, f32[64,7,7,512]{3,0,2,1:T(8,128)}, f32[64,7,7,512]{3,0,2,1:T(8,128)}, f32[64,7,7,512]{3,0,2,1:T(8,128)},...) fusion(f32[64,7,7,512]{3,0,2,1:T(8,128)} %bitcast.312), kind=kLoop, calls=%fused_computation | loop fusion | bytes 57802752 | tf_op jit(solution)/shard_map/jvp()/slice | solution.py:41
  1087.5 50.2 %multiply_reduce_fusion.25 = (f32[128]{0:T(128)S(1)}, f32[64,49,128]{2,0,1:T(8,128)}) fusion(f32[64]{0:T(128)S(1)} %get-tuple-element.283, f32[64,49,4608]{2,0,1:T(8,128)} %constant_dynamic-update-slice_fusion.36, f32[4608,128]{1,0:T(8,128)S(1)} %copy-done), kind=kOutput, calls=%fused_computation.172 | convolution fusion | flops 22197059584 | bytes 61768448 | tf_op jit(solution)/shard_map/dot_general | solution.py:21
  1137.8 21.5 psum.360
  1179.9 24.4 fusion.24
  1204.3 181.7 %reduce-scatter.8.cloned.1.call-done = f32[64,49,512]{2,0,1:T(8,128)} async-done(((f32[64,49,2048]{2,0,1:T(8,128)}), f32[64,49,512]{2,0,1:T(8,128)}) %reduce-scatter.8.cloned.1.call-update) | async-done | bytes 6422544 | tf_op jit(solution)/shard_map/reduce_scatter | solution.py:97
  1389.6 21.4 psum.362
  1446.1 19.1 psum.364
  1493.4 155.6 %all-gather.12.cloned.1.call-done = f32[64,49,2048]{2,0,1:T(8,128)} async-done(((f32[64,49,512]{2,0,1:T(8,128)}), f32[64,49,2048]{2,0,1:T(8,128)}) %all-gather.12.cloned.1.call-update) | async-done | bytes 25690128 | tf_op jit(solution)/shard_map/all_gather | solution.py:93
  1649.0 25.3 multiply_reduce_fusion.14
  1674.3 21.3 psum.366
  1714.2 50.6 %fusion.2 = f32[64,49,4608]{2,0,1:T(8,128)} fusion(f32[4608,128]{1,0:T(8,128)S(1)} %copy-done, f32[64,49,128]{2,0,1:T(8,128)} %get-tuple-element.294, f32[64,49,128]{2,0,1:T(8,128)} %get-tuple-element.293, f32[128]{0:T(128)S(1)} %broadcast_divide_fusion.7, f32[128]{0:T(128)S(1)} %get-tuple-element.137, f32[128]{0:T(128)S(1)} %get-tuple-element.141, ...), kind=kOutput, calls=%fused_computation.87 | convolution fusion | flops 22199066624 | bytes 63376128 | tf_op jit(solution)/shard_map/dot_general | solution.py:26
  1764.8 36.6 %fusion.127 = (f32[64,49,512]{2,0,1:T(8,128)}, f32[64,49,512]{2,0,1:T(8,128)}, f32[64,49,512]{2,0,1:T(8,128)}, f32[64,49,512]{2,0,1:T(8,128)}, f32[64,49,512]{2,...) fusion(f32[64,49,4608]{2,0,1:T(8,128)} %fusion.2), kind=kLoop, calls=%fused_computation.430 | loop fusion | bytes 115605504 | tf_op jit(solution)/shard_map/transpose(jvp())/split | solution.py:48
  1830.8 57.1 %reduce-scatter.10.cloned.1.call-done = f32[64,49,128]{2,0,1:T(8,128)} async-done(((f32[64,49,512]{2,0,1:T(8,128)}), f32[64,49,128]{2,0,1:T(8,128)}) %reduce-scatter.10.cloned.1.call-update) | async-done | bytes 1605648 | tf_op jit(solution)/shard_map/reduce_scatter | solution.py:97
  1890.6 21.4 psum.368
  1930.5 24.5 fusion.37
  1955.1 181.7 %reduce-scatter.12.cloned.1.call-done = f32[64,49,512]{2,0,1:T(8,128)} async-done(((f32[64,49,2048]{2,0,1:T(8,128)}), f32[64,49,512]{2,0,1:T(8,128)}) %reduce-scatter.12.cloned.1.call-update) | async-done | bytes 6422544 | tf_op jit(solution)/shard_map/reduce_scatter | solution.py:97
  2151.2 21.4 psum.370
  2173.3 17.3 psum.371
  2201.7 155.0 %all-gather.14.cloned.1.call-done = f32[64,49,2048]{2,0,1:T(8,128)} async-done(((f32[64,49,512]{2,0,1:T(8,128)}), f32[64,49,2048]{2,0,1:T(8,128)}) %all-gather.14.cloned.1.call-update) | async-done | bytes 25690128 | tf_op jit(solution)/shard_map/all_gather | solution.py:93
  2356.7 24.8 multiply_reduce_fusion.16
  2381.5 21.4 psum.372
  2403.5 17.5 psum.373
  2499.0 98.3 %convolution_bitcast_fusion = f32[4608,128]{1,0:T(8,128)} fusion(f32[64,49,4608]{2,0,1:T(8,128)} %constant_dynamic-update-slice_fusion.36, f32[64,49,128]{2,0,1:T(8,128)S(1)} %copy-done.16, f32[64,49,128]{2,0,1:T(8,128)S(1)} %copy-done.5, f32[128]{0:T(128)S(1)} %copy-done.139, f32[128]{0:T(128)S(1)} %copy-done.129, f32[128]{0:T(128)S(1)} %copy-done.84, ...), kind=kOutput, calls=%fused_computation.34 | convolution fusion | flops 22199066624 | bytes 63376128 | tf_op jit(solution)/shard_map/dot_general | solution.py:33
  2597.3 20.3 convolution_bitcast_fusion.2
  2652.8 46.3 %convolution_bitcast_fusion.1 = f32[2048,128]{1,0:T(8,128)} fusion(f32[64,49,2048]{2,0,1:T(8,128)} %all-gather.8.cloned.1.call-done, f32[64,49,128]{2,0,1:T(8,128)S(1)} %copy-done.10, f32[128]{0:T(128)S(1)} %broadcast_divide_fusion.6, f32[128]{0:T(128)S(1)} %get-tuple-element.135, f32[128]{0:T(128)S(1)} %copy-done.113, f32[128]{0:T(128)S(1)} %copy-done.111, ...), kind=kOutput, calls=%fused_computation.82 | convolution fusion | flops 9869819904 | bytes 29953280 | tf_op jit(solution)/shard_map/dot_general | solution.py:33
  2699.1 20.4 convolution_bitcast_fusion.3
  2758.9 29.1 psum.374
  2799.9 19.1 psum.375
  2819.8 34.6 %all-reduce.90 = (f32[128]{0:T(128)S(1)}, f32[128]{0:T(128)}, f32[128]{0:T(128)}, f32[128,32]{0,1:T(8,128)}, f32[9,32]{1,0:T(8,128)}, /*index=5*/f32[32,128]{1,0...) all-reduce(f32[128]{0:T(128)S(1)} %get-tuple-element.125, ...), channel_id=1, replica_groups=mesh['dp'=8,'tensor'=4] {'dp'}, use_global_device_ids=true, to_apply=%region_63.64 | all-reduce | flops 12192 | bytes 97536 | tf_op jit(solution)/shard_map/psum | solution.py:101
  2855.0 27.6 convolution_bitcast_fusion.4
  2882.6 21.8 convolution_bitcast_fusion.5
  2905.7 24.7 fusion.43
  2931.0 211.4 %all-reduce.98.cloned.1.call-done = (f32[2048,128]{0,1:T(8,128)}, f32[1,1152,128]{2,1,0:T(8,128)}, f32[128,2048]{1,0:T(8,128)}, f32[2048,128]{1,0:T(8,128)}, f32[4608,128]{1,0:T(8,128)}, /*index=5*/f32[128,2048]{1,0:T(8,128)}) async-done(((f32[2048,128]{0,1:T(8,128)}, f32[1,1152,128]{2,1,0:T(8,128)}, f32[128,2048]{1,0:T(8,128)}, f32[2048,128]{1,0:T(8,128)}, f32[4608,128]{1,0:T(8,128)}, ...) | async-done | bytes 7143440 | tf_op jit(solution)/shard_map/psum | solution.py:324
  3144.9 182.6 %reduce-scatter.14.cloned.1.call-done = f32[64,49,512]{2,0,1:T(8,128)} async-done(((f32[64,49,2048]{2,0,1:T(8,128)}), f32[64,49,512]{2,0,1:T(8,128)}) %reduce-scatter.14.cloned.1.call-update) | async-done | bytes 6422544 | tf_op jit(solution)/shard_map/reduce_scatter | solution.py:97
  (607 shorter events, 622.1 us)
Async XLA Ops:
  7.2 1080.3 %copy-start = (f32[4608,128]{1,0:T(8,128)S(1)}, f32[4608,128]{1,0:T(8,128)}, u32[]{:S(2)}) copy-start(f32[4608,128]{1,0:T(8,128)} %param.45) | copy-start | bytes 7077892
  7.2 162.9 %copy-start.61 = (f32[2048,128]{1,0:T(8,128)S(1)}, f32[2048,128]{1,0:T(8,128)}, u32[]{:S(2)}) copy-start(f32[2048,128]{1,0:T(8,128)} %param.28) | copy-start | bytes 3145732
  7.3 162.8 %all-gather.6.cloned.1.call-start = ((), (), s32[]{:S(2)}) async-start(), calls=%async_computation.5 | async-start | bytes 32112640 | tf_op jit(solution)/shard_map/all_gather | solution.py:93
  8.0 268.7 %all-reduce.96.cloned.1.call-start = ((), (), s32[]{:S(2)}) async-start(), calls=%async_computation.6 | async-start | bytes 1605632 | tf_op jit(solution)/shard_map/psum | solution.py:158
  9.5 386.8 %copy-start.75 = (f32[64]{0:T(128)}, f32[64]{0:T(128)S(1)}, u32[]{:S(2)}) copy-start(f32[64]{0:T(128)S(1)} %get-tuple-element.282) | copy-start | bytes 772
  9.5 386.9 %copy-start.105 = (f32[64]{0:T(128)}, f32[64]{0:T(128)S(1)}, u32[]{:S(2)}) copy-start(f32[64]{0:T(128)S(1)} %get-tuple-element.281) | copy-start | bytes 772
  9.5 271.1 %copy-start.142 = (f32[32]{0:T(128)}, f32[32]{0:T(128)S(1)}, u32[]{:S(2)}) copy-start(f32[32]{0:T(128)S(1)} %get-tuple-element.275) | copy-start | bytes 388
  9.5 271.1 %copy-start.146 = (f32[32]{0:T(128)}, f32[32]{0:T(128)S(1)}, u32[]{:S(2)}) copy-start(f32[32]{0:T(128)S(1)} %get-tuple-element.274) | copy-start | bytes 388
  9.5 271.1 %copy-start.155 = (f32[32]{0:T(128)}, f32[32]{0:T(128)S(1)}, u32[]{:S(2)}) copy-start(f32[32]{0:T(128)S(1)} %get-tuple-element.272) | copy-start | bytes 388
  9.5 271.1 %copy-start.157 = (f32[32]{0:T(128)}, f32[32]{0:T(128)S(1)}, u32[]{:S(2)}) copy-start(f32[32]{0:T(128)S(1)} %get-tuple-element.273) | copy-start | bytes 388
  9.5 272.2 %copy-start.140 = (f32[32]{0:T(128)}, f32[32]{0:T(128)S(1)}, u32[]{:S(2)}) copy-start(f32[32]{0:T(128)S(1)} %get-tuple-element.270) | copy-start | bytes 388
  9.5 272.1 %copy-start.144 = (f32[32]{0:T(128)}, f32[32]{0:T(128)S(1)}, u32[]{:S(2)}) copy-start(f32[32]{0:T(128)S(1)} %get-tuple-element.277) | copy-start | bytes 388
  9.5 272.1 %copy-start.148 = (f32[32]{0:T(128)}, f32[32]{0:T(128)S(1)}, u32[]{:S(2)}) copy-start(f32[32]{0:T(128)S(1)} %get-tuple-element.276) | copy-start | bytes 388
  9.6 272.1 %copy-start.151 = (f32[32]{0:T(128)}, f32[32]{0:T(128)S(1)}, u32[]{:S(2)}) copy-start(f32[32]{0:T(128)S(1)} %get-tuple-element.269) | copy-start | bytes 388
  9.6 272.1 %copy-start.153 = (f32[32]{0:T(128)}, f32[32]{0:T(128)S(1)}, u32[]{:S(2)}) copy-start(f32[32]{0:T(128)S(1)} %get-tuple-element.271) | copy-start | bytes 388
  217.0 178.4 %copy-start.71 = (f32[128]{0:T(128)}, f32[128]{0:T(128)S(1)}, u32[]{:S(2)}) copy-start(f32[128]{0:T(128)S(1)} %broadcast_divide_fusion.11) | copy-start | bytes 1540
  237.7 157.7 %copy-start.73 = (f32[128]{0:T(128)}, f32[128]{0:T(128)S(1)}, u32[]{:S(2)}) copy-start(f32[128]{0:T(128)S(1)} %get-tuple-element.147) | copy-start | bytes 1540
  244.1 440.0 %reduce-scatter.6.cloned.1.call-start = ((), (), s32[]{:S(2)}) async-start(), calls=%async_computation.7 | async-start | bytes 32112640 | tf_op jit(solution)/shard_map/reduce_scatter | solution.py:97
  306.7 4.4 collective-permute-start
  331.7 21.0 collective-permute-start.1
  373.3 22.1 collective-permute-start.2
  483.5 414.0 %all-gather.8.cloned.1.call-start = ((), (), s32[]{:S(2)}) async-start(), calls=%async_computation.8 | async-start | bytes 32112640 | tf_op jit(solution)/shard_map/all_gather | solution.py:93
  741.8 271.6 %all-gather.10.cloned.1.call-start = ((), (), s32[]{:S(2)}) async-start(), calls=%async_computation.9 | async-start | bytes 8028160 | tf_op jit(solution)/shard_map/all_gather | solution.py:93
  967.5 418.5 %reduce-scatter.8.cloned.1.call-start = ((), (), s32[]{:S(2)}) async-start(), calls=%async_computation.10 | async-start | bytes 32112640 | tf_op jit(solution)/shard_map/reduce_scatter | solution.py:97
  1159.9 554.2 %copy-start.81 = (f32[128]{0:T(128)}, f32[128]{0:T(128)S(1)}, u32[]{:S(2)}) copy-start(f32[128]{0:T(128)S(1)} %broadcast_divide_fusion.8) | copy-start | bytes 1540
  1179.9 534.3 %copy-start.83 = (f32[128]{0:T(128)}, f32[128]{0:T(128)S(1)}, u32[]{:S(2)}) copy-start(f32[128]{0:T(128)S(1)} %get-tuple-element.141) | copy-start | bytes 1540
  1204.3 444.7 %all-gather.12.cloned.1.call-start = ((), (), s32[]{:S(2)}) async-start(), calls=%async_computation.11 | async-start | bytes 32112640 | tf_op jit(solution)/shard_map/all_gather | solution.py:93
  1493.4 394.5 %reduce-scatter.10.cloned.1.call-start = ((), (), s32[]{:S(2)}) async-start(), calls=%async_computation.12 | async-start | bytes 8028160 | tf_op jit(solution)/shard_map/reduce_scatter | solution.py:97
  1830.7 306.0 %reduce-scatter.12.cloned.1.call-start = ((), (), s32[]{:S(2)}) async-start(), calls=%async_computation.13 | async-start | bytes 32112640 | tf_op jit(solution)/shard_map/reduce_scatter | solution.py:97
  1955.0 181.8 %copy-start.86 = (f32[512]{0:T(512)S(1)}, f32[512]{0:T(512)}, u32[]{:S(2)}) copy-start(f32[512]{0:T(512)} %copy-done.85) | copy-start | bytes 6148
  1955.0 181.8 %copy-start.98 = (f32[512]{0:T(512)S(1)}, f32[512]{0:T(512)}, u32[]{:S(2)}) copy-start(f32[512]{0:T(512)} %copy-done.97) | copy-start | bytes 6148
  1955.0 181.8 %copy-start.115 = (f32[512]{0:T(512)S(1)}, f32[512]{0:T(512)}, u32[]{:S(2)}) copy-start(f32[512]{0:T(512)} %param.40) | copy-start | bytes 6148
  1955.0 181.8 %copy-start.131 = (f32[512]{0:T(512)S(1)}, f32[512]{0:T(512)}, u32[]{:S(2)}) copy-start(f32[512]{0:T(512)} %param.41) | copy-start | bytes 6148
  1955.0 195.6 %copy-start.109 = (f32[512]{0:T(512)S(1)}, f32[512]{0:T(512)}, u32[]{:S(2)}) copy-start(f32[512]{0:T(512)} %copy-done.108) | copy-start | bytes 6148
  1955.0 217.6 %copy-start.136 = (f32[512]{0:T(512)S(1)}, f32[512]{0:T(512)}, u32[]{:S(2)}) copy-start(f32[512]{0:T(512)} %get-tuple-element.56) | copy-start | bytes 6148
  1955.1 401.6 %all-gather.14.cloned.1.call-start = ((), (), s32[]{:S(2)}) async-start(), calls=%async_computation.14 | async-start | bytes 32112640 | tf_op jit(solution)/shard_map/all_gather | solution.py:93
  2200.9 155.7 %copy-start.7 = (f32[64,49,128]{2,0,1:T(8,128)S(1)}, f32[64,49,128]{2,0,1:T(8,128)}, u32[]{:S(2)}) copy-start(f32[64,49,128]{2,0,1:T(8,128)} %get-tuple-element.289) | copy-start | bytes 4816900
  2200.9 155.7 %copy-start.60 = (f32[128,2048]{1,0:T(8,128)S(1)}, f32[128,2048]{1,0:T(8,128)}, u32[]{:S(2)}) copy-start(f32[128,2048]{1,0:T(8,128)} %param.39) | copy-start | bytes 3145732
  2200.9 155.7 %copy-start.100 = (f32[128]{0:T(128)S(1)}, f32[128]{0:T(128)}, u32[]{:S(2)}) copy-start(f32[128]{0:T(128)} %copy-done.99) | copy-start | bytes 1540
  2201.0 941.4 %all-reduce.98.cloned.1.call-start = ((), (), s32[]{:S(2)}) async-start(), calls=%async_computation.16 | async-start | bytes 14286848 | tf_op jit(solution)/shard_map/psum | solution.py:324
  2201.7 179.8 %copy-start.172 = (f32[128]{0:T(128)S(1)}, f32[128]{0:T(128)}, u32[]{:S(2)}) copy-start(f32[128]{0:T(128)} %get-tuple-element.146) | copy-start | bytes 1540
  2201.7 201.2 %copy-start.168 = (f32[128]{0:T(128)S(1)}, f32[128]{0:T(128)}, u32[]{:S(2)}) copy-start(f32[128]{0:T(128)} %get-tuple-element.77) | copy-start | bytes 1540
  2424.3 295.3 %copy-start.4 = (f32[64,49,128]{2,0,1:T(8,128)}, f32[64,49,128]{2,0,1:T(8,128)S(1)}, u32[]{:S(2)}) copy-start(f32[64,49,128]{2,0,1:T(8,128)S(1)} %multiply_add_fusion.3) | copy-start | bytes 4816900
  2458.1 5.4 collective-permute-start.3
  2497.5 120.1 %collective-permute-start.4 = (f32[64,49,128]{2,0,1:T(8,128)S(1)}, f32[64,49,128]{2,0,1:T(8,128)S(1)}, u32[]{:S(2)}, u32[]{:S(2)}) collective-permute-start(f32[64,49,128]{2,0,1:T(8,128)S(1)} %pad_add_fusion.36), channel_id=1, source_target_pairs={{1,0},{2,1},{3,2},{5,4},{6,5},{7,6},{9,8},{10,9},{11,10},{13,12},{... | collective-permute-start | bytes 4816904 | tf_op jit(solution)/shard_map/ppermute | solution.py:16
  2651.2 68.3 %collective-permute-start.5 = (f32[64,49,128]{2,0,1:T(8,128)S(1)}, f32[64,49,128]{2,0,1:T(8,128)S(1)}, u32[]{:S(2)}, u32[]{:S(2)}) collective-permute-start(f32[64,49,128]{2,0,1:T(8,128)S(1)} %pad_add_fusion.35), channel_id=1, source_target_pairs={{1,0},{2,1},{3,2},{5,4},{6,5},{7,6},{9,8},{10,9},{11,10},{13,12},{... | collective-permute-start | bytes 4816904 | tf_op jit(solution)/shard_map/ppermute | solution.py:16
  2904.5 423.1 %reduce-scatter.14.cloned.1.call-start = ((), (), s32[]{:S(2)}) async-start(), calls=%async_computation.15 | async-start | bytes 32112640 | tf_op jit(solution)/shard_map/reduce_scatter | solution.py:97
  3144.9 192.2 %copy-start.70 = (f32[1,1152,128]{2,1,0:T(8,128)S(1)}, f32[1,1152,128]{2,1,0:T(8,128)}, u32[]{:S(2)}) copy-start(f32[1,1152,128]{2,1,0:T(8,128)} %get-tuple-element.309) | copy-start | bytes 1769476
  (161 other events, 3429.3 us)
Sparse Core Ops, SparseCore 0:
  9.7 160.3 all-gather.5
  244.2 32.3 all-reduce.95
  483.6 200.5 reduce-scatter.5
  741.9 155.4 all-gather.7
  967.6 45.7 all-gather.9
  1204.4 181.5 reduce-scatter.7
  1493.5 155.4 all-gather.11
  1830.8 57.0 reduce-scatter.9
  1955.2 181.5 reduce-scatter.11
  2201.1 155.4 all-gather.13
  2904.6 237.7 all-reduce.97
  3144.8 182.6 reduce-scatter.13
where the time goes:
time: 3360 us; the launch traced here: 3350 us
  waiting for transfers between devices  1730 us (51%)
  matrix products  656 us (20%)
  blocking collectives  506 us (15%)
  local copies, waits for them, and re-layouts  206 us (6%)
  other arithmetic  188 us (6%)
  starting transfers between devices  45.1 us (1%)
    reduce_scatter x5, waiting for transfers between devices, channels_part(): return lax.psum_scatter(values, 'tensor', scatter_dimension=2, tiled=True)  804 us
    all_gather x5, waiting for transfers between devices, channels_all(): return lax.all_gather(values, 'tensor', axis=2, tiled=True)  672 us
    psum x24, blocking collectives, batch_total(): return lax.psum(values, 'dp')  477 us
    dot_general x15, matrix products, dense(): jnp.dot(flat, weight, precision=HIGH)  293 us
    psum x1, waiting for transfers between devices, local(): lax.psum((grads[0], grads[1], grads[2], grads[3], grads[4], grads[5], gra...  211 us
    dot_general x6, matrix products, weight_grad(): lax.dot_general(flat_left, flat_right, (((0,), (0,)), ((), ())), precisio...  208 us
    dot_general x6, matrix products, back_dense(): lax.dot_general(flat, weight, (((1,), (1,)), ((), ())), precision=HIGH)  154 us
    split x5, local copies, waits for them, and re-layouts, stack_taps(): return jnp.concatenate(frame_taps(values), axis=-1)  80 us
  transfers between devices with their start and end apart: 18, of which 16 were waited for; matrix products, arithmetic and copies ran while one was open for 6% of the time, Pallas kernels for 0%

commit v1 on v0

v1 whole, which is shorter than its diff:
```python
import jax
import jax.numpy as jnp
import numpy as np
from jax import lax
from jax.sharding import PartitionSpec as P

SIDE = 7
CELLS = SIDE * SIDE
EPS = 1e-05
FWD = lax.Precision.HIGHEST
BWD = lax.Precision.HIGH
GRAD = lax.Precision.DEFAULT
BOTH = ("dp", "tensor")


def edge_mask():
    mask = np.zeros((CELLS, 9), np.float32)
    for row in range(SIDE):
        for col in range(SIDE):
            for a in range(3):
                for b in range(3):
                    if 0 <= row - (a - 1) < SIDE and 0 <= col - (b - 1) < SIDE:
                        mask[row * SIDE + col, a * 3 + b] = 1.0
    return mask


def mm(values, weight, precision):
    return lax.dot_general(values, weight, (((values.ndim - 1,), (0,)), ((), ())), precision=precision)


def mm_t(values, weight, precision):
    return lax.dot_general(values, weight, (((values.ndim - 1,), (1,)), ((), ())), precision=precision)


def outer(left, right, precision):
    return lax.dot_general(left, right, (((0, 1), (0, 1)), ((), ())), precision=precision)


def stack9(x):
    cells, frames, chans = x.shape
    grid = jnp.pad(x.reshape(SIDE, SIDE, frames, chans), ((1, 1), (1, 1), (0, 0), (0, 0)))
    return jnp.concatenate(
        [
            grid[row : row + SIDE, col : col + SIDE].reshape(cells, frames, chans)
            for row in range(3)
            for col in range(3)
        ],
        axis=-1,
    )


def flip_taps(weight, chans):
    outs = weight.shape[1]
    return weight.reshape(9, chans, outs)[::-1].transpose(0, 2, 1).reshape(9 * outs, chans)


def moments(h, mask, count, axes):
    local = jnp.sum(mask) * CELLS
    total = jnp.sum(h * mask, axis=(0, 1))
    mean = total / jnp.maximum(local, 1.0)
    second = jnp.sum(mask * (h - mean) ** 2, axis=(0, 1))
    local_row = jnp.full_like(mean, local)
    all_parts = lax.all_gather(jnp.stack([mean, second, local_row]), axes)
    means, seconds, counts = all_parts[:, 0], all_parts[:, 1], all_parts[:, 2]
    mean = jnp.sum(means * counts, axis=0) / count
    var = (jnp.sum(seconds, axis=0) + jnp.sum(counts * (means - mean) ** 2, axis=0)) / count
    return mean, lax.rsqrt(var + EPS)


def norm_back(grad, xhat, mask, gain, rstd, count, axes):
    sums = jnp.stack([jnp.sum(grad, axis=(0, 1)), jnp.sum(grad * xhat, axis=(0, 1))])
    sums = lax.psum(sums, axes)
    back = gain * rstd * (grad - mask * (sums[0] + xhat * sums[1]) / count)
    return back, sums[1], sums[0]


def reduce_frames(partial):
    return lax.psum_scatter(partial, "tensor", scatter_dimension=1, tiled=True)


def gather_frames(part):
    return lax.all_gather(part, "tensor", axis=1, tiled=True)


def shift_from(value, steps):
    count = lax.axis_size("tensor")
    initial, last = (max(0, -steps), min(count, count - steps))
    return lax.ppermute(value, "tensor", [(s, s + steps) for s in range(initial, last)])


def halo(x, width):
    left = shift_from(x[:, x.shape[1] - width :], 1)
    right = shift_from(x[:, :width], -1)
    return jnp.concatenate([left, x, right], axis=1)


def later(x):
    return jnp.concatenate([x[:, 1:], jnp.zeros_like(x[:, :1])], axis=1)


def earlier(x):
    return jnp.concatenate([jnp.zeros_like(x[:, :1]), x[:, :-1]], axis=1)


def local(
    features, frame_clip, reduce_first, gain_reduce, bias_reduce, motion_down, motion_kernel, motion_up,
    motion_bias, group_taps, group_spatial, gain_groups, bias_groups, expand_first, gain_expand, bias_expand,
    reduce_second, gain_narrow, bias_narrow, spatial_second, gain_spatial, bias_spatial, expand_second,
    gain_output, bias_output, cotangent,
):
    tensor = lax.axis_size("tensor")
    at = lax.axis_index("tensor")
    frames = features.shape[0]
    own = frames // tensor
    gw = group_taps.shape[2]
    rank = motion_down.shape[1]
    groups = tensor
    reach = groups
    x = jnp.transpose(features, (1, 0, 2))
    seed = jnp.transpose(cotangent, (1, 0, 2))

    valid = (frame_clip >= 0).astype(jnp.float32)
    count = lax.psum(jnp.sum(valid) * CELLS, "dp")
    wide_mask = valid[None, :, None]
    padded = jnp.pad(frame_clip, (reach + 1, reach + 1), constant_values=-2)
    clips = lax.dynamic_slice(padded, (at * own,), (own + 2 * reach + 2,))
    here = clips[1:-1]
    next_ext = ((here >= 0) & (clips[2:] == here)).astype(jnp.float32)[None, :, None]
    prev_ext = ((here >= 0) & (clips[:-2] == here)).astype(jnp.float32)[None, :, None]
    mask = (here >= 0).astype(jnp.float32)[reach : reach + own][None, :, None]
    next_own = next_ext[0, reach : reach + own]

    rows = lambda w: lax.all_to_all(w, "tensor", 0, 1, tiled=True)
    cols = lambda w: lax.all_to_all(w, "tensor", 1, 0, tiled=True)
    w_reduce, w_reduce2 = rows(reduce_first), rows(reduce_second)
    w_expand, w_expand2 = cols(expand_first), cols(expand_second)
    small = jnp.concatenate(
        [
            motion_down.T, motion_up, motion_bias[None], gain_reduce[None], bias_reduce[None], gain_groups[None],
            bias_groups[None], gain_narrow[None], bias_narrow[None], gain_spatial[None], bias_spatial[None],
            group_taps[0],
        ],
        axis=0,
    )
    small = lax.all_gather(small, "tensor", axis=1, tiled=True)
    md, mu = small[:rank].T, small[rank : 2 * rank]
    mb, g_red, b_red, g_grp, b_grp, g_nar, b_nar, g_spa, b_spa = [small[2 * rank + i] for i in range(9)]
    taps = small[2 * rank + 9 : 2 * rank + 12]
    spatial = lax.all_gather(spatial_second, "tensor", axis=1, tiled=True)
    group_w = lax.all_gather(group_spatial, "tensor", axis=0, tiled=True)

    h1 = reduce_frames(mm(x, w_reduce, FWD))
    mean1, r1 = moments(h1, mask, count, BOTH)
    xh1 = (h1 - mean1) * r1
    n1 = g_red * xh1 + b_red
    act1 = jnp.maximum(n1, 0.0)

    edges = jnp.asarray(edge_mask())
    w_pos = jnp.sum(edges[:, :, None] * motion_kernel[None], axis=1)
    motion = mm(act1, md, FWD)
    ahead = jnp.sum(motion * w_pos[:, None, :], axis=0)
    base = jnp.sum(motion, axis=0)
    follow = jnp.concatenate([ahead[1:], shift_from(ahead[:1], -1)], axis=0)
    pooled = next_own * (follow - base) / CELLS
    gate = jax.nn.sigmoid(jnp.dot(pooled, mu, precision=FWD) + mb)
    excited = act1 * gate[None]
    exc = halo(excited, reach)
    ins, mids, outs = [], [], []
    carry = 0.0
    mine = slice(reach, reach + own)
    for g in range(groups):
        part = slice(g * gw, (g + 1) * gw)
        u = exc[:, :, part] + carry
        k = taps[:, part]
        stacked = stack9(k[0] * earlier(u) * prev_ext + k[1] * u + k[2] * later(u) * next_ext)
        carry = mm(stacked, group_w[g], FWD)
        ins.append(u)
        mids.append(stacked[:, mine])
        outs.append(carry[:, mine])
    grouped = jnp.concatenate(outs, axis=-1)
    mean2, r2 = moments(grouped, mask, count, BOTH)
    xh2 = (grouped - mean2) * r2
    n2 = g_grp * xh2 + b_grp
    mixed = gather_frames(jnp.maximum(n2, 0.0))
    h3 = mm(mixed, w_expand, FWD)
    mean3, r3 = moments(h3, wide_mask, count, "dp")
    xh3 = (h3 - mean3) * r3
    pre3 = gain_expand * xh3 + bias_expand + x
    middle = jnp.maximum(pre3, 0.0)

    h4 = reduce_frames(mm(middle, w_reduce2, FWD))
    mean4, r4 = moments(h4, mask, count, BOTH)
    xh4 = (h4 - mean4) * r4
    n4 = g_nar * xh4 + b_nar
    stacked4 = stack9(jnp.maximum(n4, 0.0))
    h5 = mm(stacked4, spatial, FWD)
    mean5, r5 = moments(h5, mask, count, BOTH)
    xh5 = (h5 - mean5) * r5
    n5 = g_spa * xh5 + b_spa
    conv_act = gather_frames(jnp.maximum(n5, 0.0))
    h6 = mm(conv_act, w_expand2, FWD)
    mean6, r6 = moments(h6, wide_mask, count, "dp")
    xh6 = (h6 - mean6) * r6
    pre6 = gain_output * xh6 + bias_output + middle
    output = wide_mask * jnp.maximum(pre6, 0.0)

    d_last = jnp.where(pre6 > 0, seed * wide_mask, 0.0)
    d6, gg_output, gb_output = norm_back(d_last, xh6, wide_mask, gain_output, r6, count, "dp")
    gw_expand2 = outer(conv_act, d6, GRAD)
    d_n5 = jnp.where(n5 > 0, reduce_frames(mm_t(d6, w_expand2, BWD)), 0.0)
    d5, gg_spa, gb_spa = norm_back(d_n5, xh5, mask, g_spa, r5, count, BOTH)
    gw_spatial = outer(stacked4, d5, GRAD)
    d_n4 = jnp.where(n4 > 0, mm(stack9(d5), flip_taps(spatial, d5.shape[2]), BWD), 0.0)
    d4, gg_nar, gb_nar = norm_back(d_n4, xh4, mask, g_nar, r4, count, BOTH)
    d4_all = gather_frames(d4) * wide_mask
    gw_reduce2 = outer(middle, d4_all, GRAD)
    d_pre3 = jnp.where(pre3 > 0, d_last + mm_t(d4_all, w_reduce2, BWD), 0.0)

    d3, gg_expand, gb_expand = norm_back(d_pre3, xh3, wide_mask, gain_expand, r3, count, "dp")
    gw_expand = outer(mixed, d3, GRAD)
    d_n2 = jnp.where(n2 > 0, reduce_frames(mm_t(d3, w_expand, BWD)), 0.0)
    d2, gg_grp, gb_grp = norm_back(d_n2, xh2, mask, g_grp, r2, count, BOTH)
    d2_ext = halo(d2, reach)
    d_exc, gw_group, g_taps = [None] * groups, [None] * groups, [None] * groups
    carry = 0.0
    for g in reversed(range(groups)):
        part = slice(g * gw, (g + 1) * gw)
        k = taps[:, part]
        dy = d2_ext[:, :, part] + carry
        gw_group[g] = outer(mids[g], dy[:, mine], GRAD)
        dt = mm(stack9(dy), flip_taps(group_w[g], gw), BWD)
        u = ins[g]
        g_taps[g] = jnp.stack(
            [
                jnp.sum((dt * prev_ext * earlier(u))[:, mine], axis=(0, 1)),
                jnp.sum((dt * u)[:, mine], axis=(0, 1)),
                jnp.sum((dt * next_ext * later(u))[:, mine], axis=(0, 1)),
            ]
        )
        carry = k[0] * later(dt * prev_ext) + k[1] * dt + k[2] * earlier(dt * next_ext)
        d_exc[g] = carry[:, mine]
    d_exc = jnp.concatenate(d_exc, axis=-1)
    d_gate = jnp.sum(d_exc * act1, axis=0) * gate * (1.0 - gate)
    g_mb = jnp.sum(d_gate, axis=0)
    g_mu = lax.dot_general(pooled, d_gate, (((0,), (0,)), ((), ())), precision=FWD)
    d_pool = mm_t(d_gate, mu, FWD) * next_own / CELLS
    d_ahead = jnp.concatenate([shift_from(d_pool[-1:], 1), d_pool[:-1]], axis=0)
    g_pos = jnp.sum(motion * d_ahead[None], axis=1)
    g_mk = jnp.sum(edges[:, :, None] * g_pos[:, None, :], axis=0)
    d_motion = w_pos[:, None, :] * d_ahead[None] - d_pool[None]
    g_md = outer(act1, d_motion, FWD)
    d_n1 = jnp.where(n1 > 0, d_exc * gate[None] + mm_t(d_motion, md, FWD), 0.0)
    d1, gg_red, gb_red = norm_back(d_n1, xh1, mask, g_red, r1, count, BOTH)
    d1_all = gather_frames(d1) * wide_mask
    gw_reduce = outer(x, d1_all, GRAD)
    grad_features = d_pre3 + mm_t(d1_all, w_reduce, BWD)

    gw_spatial = lax.psum_scatter(gw_spatial, "tensor", scatter_dimension=1, tiled=True)
    gw_group = lax.psum_scatter(jnp.stack(gw_group), "tensor", scatter_dimension=0, tiled=True)
    big = lax.psum(
        (cols(gw_reduce), rows(gw_expand), cols(gw_reduce2), rows(gw_expand2), gw_spatial, gw_group), "dp"
    )
    tiny = jnp.concatenate([g_md.T, g_mu, g_mb[None], jnp.concatenate(g_taps, axis=-1)], axis=0)
    tiny, g_mk = lax.psum((tiny, g_mk), BOTH)
    narrow = jnp.stack([gg_red, gb_red, gg_grp, gb_grp, gg_nar, gb_nar, gg_spa, gb_spa])
    tiny = lax.dynamic_slice(jnp.concatenate([tiny, narrow]), (0, at * gw), (2 * rank + 12, gw))
    vec = tiny[2 * rank + 4 :]
    return (
        jnp.transpose(output, (1, 0, 2)),
        jnp.transpose(grad_features, (1, 0, 2)),
        big[0],
        vec[0],
        vec[1],
        tiny[:rank].T,
        g_mk,
        tiny[rank : 2 * rank],
        tiny[2 * rank],
        tiny[2 * rank + 1 : 2 * rank + 4][None],
        big[5],
        vec[2],
        vec[3],
        big[1],
        gg_expand,
        gb_expand,
        big[2],
        vec[4],
        vec[5],
        big[4],
        vec[6],
        vec[7],
        big[3],
        gg_output,
        gb_output,
    )


def solution(mesh):
    wide, col, row, chan, deep = P("dp", None, "tensor"), P(None, "tensor"), P("tensor", None), P("tensor"), P("tensor", None, None)
    return jax.shard_map(
        local,
        mesh=mesh,
        in_specs=(wide, P("dp"), col, chan, chan, row, P(), col, chan, deep, deep, chan, chan, row, chan, chan, col, chan, chan, col, chan, chan, row, chan, chan, wide),
        out_specs=(wide, wide, col, chan, chan, row, P(), col, chan, deep, deep, chan, chan, row, chan, chan, col, chan, chan, col, chan, chan, row, chan, chan),
        check_vma=False,
    )
```

time: 3360 us -> 1790 us (0.53)
  waiting for transfers between devices: 1730 us -> 745 us
  matrix products: 656 us -> 248 us
  other arithmetic: 188 us -> 96.5 us
  local copies, waits for them, and re-layouts: 206 us -> 119 us
    all_gather x5 -> x6, waiting for transfers between devices: 672 us -> 83.2 us  [the longest x4 77.9 us: gather_frames(): return lax.all_gather(part, 'tensor', axis=1, tiled=True)]
    reduce_scatter x5 -> x6, waiting for transfers between devices: 804 us -> 224 us  [the longest x4 172 us: reduce_frames(): return lax.psum_scatter(partial, 'tensor', scatter_dimension=1, tiled=True)]
    dot_general x30 -> x33, matrix products: 656 us -> 248 us  [the longest x15 135 us: mm(): lax.dot_general(values, weight, (((values.ndim - 1,), (0,)), ((), ())), p...]
    psum x25 -> x7, blocking collectives: 506 us -> 225 us  [the longest x6 201 us: norm_back(): sums = lax.psum(sums, axes)]
    all_gather x0 -> x7, blocking collectives: none -> 234 us  [the longest x6 228 us: moments(): all_parts = lax.all_gather(jnp.stack([mean, second, local_row]), axes)]
    psum x2, waiting for transfers between devices: 244 us -> 343 us  [the longest x1 225 us: local(): lax.psum((cols(gw_reduce), rows(gw_expand), cols(gw_reduce2), rows(gw_exp...]
    all_to_all x0 -> x6, waiting for transfers between devices: none -> 89.5 us  [the longest x3 58.7 us: local(): cols = lambda w: lax.all_to_all(w, 'tensor', 1, 0, tiled=True)]
    split x6 -> x0, local copies, waits for them, and re-layouts: 80 us -> none  [the longest x5 80 us: stack_taps(): return jnp.concatenate(frame_taps(values), axis=-1)]
  transfers between devices with their start and end apart: 18 -> 26, of which waited for: 16 -> 21; matrix products, arithmetic and copies ran while one was open for 6% -> 11% of each run, Pallas kernels for 0% -> 0%
where the time goes in v1:
time: 1790 us; the launch traced here: 1780 us
  waiting for transfers between devices  745 us (42%)
  blocking collectives  507 us (28%)
  matrix products  248 us (14%)
  local copies, waits for them, and re-layouts  119 us (7%)
  other arithmetic  96.5 us (5%)
  starting transfers between devices  40.6 us (2%)
  between operations  19.1 us (1%)
    all_gather x6, blocking collectives, moments(): all_parts = lax.all_gather(jnp.stack([mean, second, local_row]), axes)  228 us
    psum x1, waiting for transfers between devices, local(): lax.psum((cols(gw_reduce), rows(gw_expand), cols(gw_reduce2), rows(gw_exp...  225 us
    psum x6, blocking collectives, norm_back(): sums = lax.psum(sums, axes)  201 us
    reduce_scatter x4, waiting for transfers between devices, reduce_frames(): return lax.psum_scatter(partial, 'tensor', scatter_dimension=1, tiled=True)  172 us
    dot_general x15, matrix products, mm(): lax.dot_general(values, weight, (((values.ndim - 1,), (0,)), ((), ())), p...  135 us
    psum x1, waiting for transfers between devices, local(): tiny, g_mk = lax.psum((tiny, g_mk), BOTH)  117 us
    all_gather x4, waiting for transfers between devices, gather_frames(): return lax.all_gather(part, 'tensor', axis=1, tiled=True)  77.9 us
    all_to_all x3, waiting for transfers between devices, local(): cols = lambda w: lax.all_to_all(w, 'tensor', 1, 0, tiled=True)  58.7 us
  transfers between devices with their start and end apart: 26, of which 21 were waited for; matrix products, arithmetic and copies ran while one was open for 11% of the time, Pallas kernels for 0%

profile of v1, /device:TPU:0, one launch (start us, length us, event | category | flops | bytes accessed | tf_op | source)
XLA Modules:
  0.0 1775.0 jit_solution(8320388399442919134)
XLA Ops:
  7.2 18.7 %all_to_all.152 = f32[4,512,128]{2,1,0:T(8,128)S(1)} all-to-all(f32[4,512,128]{2,1,0:T(8,128)} %bitcast.632), channel_id=1, replica_groups=mesh['dp'=8,'tensor'=4] {'tensor'}, dimensions={0} | all-to-all | bytes 2097152 | tf_op jit(solution)/shard_map/all_to_all | solution.py:133
  27.1 14.6 fusion.5
  44.8 23.6 %psum.105 = f32[]{:T(128)} all-reduce(f32[]{:T(128)} %mul.939), channel_id=1, replica_groups=mesh['dp'=8,'tensor'=4] {'dp'}, use_global_device_ids=true, to_apply=%region_6.7 | all-reduce | flops 1 | bytes 8 | tf_op jit(solution)/shard_map/psum | solution.py:123
  75.9 27.3 %reduce-scatter.7.cloned.1.call-done = f32[49,16,512]{2,1,0:T(8,128)} async-done(((f32[49,64,512]{2,1,0:T(8,128)}), f32[49,16,512]{2,1,0:T(8,128)}) %reduce-scatter.7.cloned.1.call-update) | async-done | bytes 1605648 | tf_op jit(solution)/shard_map/reduce_scatter | solution.py:78
  106.7 41.4 %all-gather.6 = f32[32,3,512]{2,1,0:T(4,128)S(1)} all-gather(f32[1,3,512]{2,1,0:T(4,128)S(1)} %maximum_bitcast_fusion), channel_id=2, replica_groups=mesh['dp'=8,'tensor'=4] {'dp','tensor'}, dimensions={0}, use_global_device_ids=true | all-gather | bytes 202752 | tf_op jit(solution)/shard_map/all_gather | solution.py:63
  176.8 7.1 slice_add_fusion.5
  205.7 42.6 %all-gather.7 = f32[32,3,512]{2,1,0:T(4,128)S(1)} all-gather(f32[1,3,512]{2,1,0:T(4,128)S(1)} %maximum_bitcast_fusion.1), channel_id=3, replica_groups=mesh['dp'=8,'tensor'=4] {'dp','tensor'}, dimensions={0}, use_global_device_ids=true | all-gather | bytes 202752 | tf_op jit(solution)/shard_map/all_gather | solution.py:63
  255.9 24.6 %all-to-all-done.2 = f32[4,512,128]{2,1,0:T(8,128)S(1)} async-done(((f32[4,512,128]{2,1,0:T(8,128)}), f32[4,512,128]{2,1,0:T(8,128)S(1)}, u32[]{:S(2)}, u32[]{:S(2)}) %all-to-all-start.2) | async-done | bytes 1048608 | tf_op jit(solution)/shard_map/all_to_all | solution.py:133
  285.3 24.7 %all-to-all-done.1 = f32[128,4,512]{2,0,1:T(8,128)S(1)} async-done(((f32[128,4,512]{2,0,1:T(8,128)}), f32[128,4,512]{2,0,1:T(8,128)S(1)}, u32[]{:S(2)}, u32[]{:S(2)}) %all-to-all-start.1) | async-done | bytes 1048608 | tf_op jit(solution)/shard_map/all_to_all | solution.py:134
  316.6 14.3 multiply_reduce_fusion.5
  332.2 30.5 %all-gather.8 = f32[8,3,512]{2,1,0:T(4,128)S(1)} all-gather(f32[1,3,512]{2,1,0:T(4,128)S(1)} %maximum_bitcast_fusion.2), channel_id=4, replica_groups=mesh['dp'=8,'tensor'=4] {'dp'}, dimensions={0}, use_global_device_ids=true | all-gather | bytes 55296 | tf_op jit(solution)/shard_map/all_gather | solution.py:63
  368.6 14.4 fusion.15
  383.7 55.1 %reduce-scatter.9.cloned.1.call-done = f32[49,16,512]{2,1,0:T(8,128)} async-done(((f32[49,64,512]{2,1,0:T(8,128)}), f32[49,16,512]{2,1,0:T(8,128)}) %reduce-scatter.9.cloned.1.call-update) | async-done | bytes 1605648 | tf_op jit(solution)/shard_map/reduce_scatter | solution.py:78
  442.2 41.9 %all-gather.9 = f32[32,3,512]{2,1,0:T(4,128)S(1)} all-gather(f32[1,3,512]{2,1,0:T(4,128)S(1)} %maximum_bitcast_fusion.3), channel_id=5, replica_groups=mesh['dp'=8,'tensor'=4] {'dp','tensor'}, dimensions={0}, use_global_device_ids=true | all-gather | bytes 202752 | tf_op jit(solution)/shard_map/all_gather | solution.py:63
  507.8 26.6 %multiply_reduce_fusion.12 = (f32[512]{0:T(512)S(1)}, f32[49,16,512]{2,1,0:T(8,128)S(1)}) fusion(f32[16]{0:T(128)S(1)} %slice_convert_fusion, f32[49,16,4608]{2,1,0:T(8,128)} %constant_dynamic-update-slice_fusion.36, f32[4608,512]{1,0:T(8,128)} %all-gather.23.cloned.1.call-done), kind=kOutput, calls=%fused_computation.158 | convolution fusion | flops 22197059584 | bytes 25495616 | tf_op jit(solution)/shard_map/dot_general | solution.py:28
  534.8 41.0 %all-gather.10 = f32[32,3,512]{2,1,0:T(4,128)S(1)} all-gather(f32[1,3,512]{2,1,0:T(4,128)S(1)} %maximum_bitcast_fusion.4), channel_id=6, replica_groups=mesh['dp'=8,'tensor'=4] {'dp','tensor'}, dimensions={0}, use_global_device_ids=true | all-gather | bytes 202752 | tf_op jit(solution)/shard_map/all_gather | solution.py:63
  580.2 29.0 %all_to_all.153 = f32[128,4,512]{2,0,1:T(8,128)} all-to-all(f32[128,4,512]{2,0,1:T(8,128)S(1)} %bitcast.556), channel_id=1, replica_groups=mesh['dp'=8,'tensor'=4] {'tensor'}, dimensions={1} | all-to-all | bytes 2097152 | tf_op jit(solution)/shard_map/all_to_all | solution.py:134
  609.2 24.3 %all-gather.25.cloned.1.call-done = f32[49,64,512]{2,1,0:T(8,128)} async-done(((f32[49,16,512]{2,1,0:T(8,128)}), f32[49,64,512]{2,1,0:T(8,128)}) %all-gather.25.cloned.1.call-update) | async-done | bytes 6422544 | tf_op jit(solution)/shard_map/all_gather | solution.py:82
  633.5 14.4 multiply_reduce_fusion.3
  649.2 30.5 %all-gather.11 = f32[8,3,512]{2,1,0:T(4,128)S(1)} all-gather(f32[1,3,512]{2,1,0:T(4,128)S(1)} %maximum_bitcast_fusion.5), channel_id=7, replica_groups=mesh['dp'=8,'tensor'=4] {'dp'}, dimensions={0}, use_global_device_ids=true | all-gather | bytes 55296 | tf_op jit(solution)/shard_map/all_gather | solution.py:63
  685.7 17.1 psum.106
  712.1 7.2 fusion.157
  719.4 10.2 reverse_bitcast_fusion
  729.6 10.0 copy.148
  739.5 36.9 %reduce-scatter.11.cloned.1.call-done = f32[49,16,512]{2,1,0:T(8,128)} async-done(((f32[49,64,512]{2,1,0:T(8,128)}), f32[49,16,512]{2,1,0:T(8,128)}) %reduce-scatter.11.cloned.1.call-update) | async-done | bytes 1605648 | tf_op jit(solution)/shard_map/reduce_scatter | solution.py:78
  778.4 39.6 %psum.107 = f32[2,512]{1,0:T(2,128)S(1)} all-reduce(f32[2,512]{1,0:T(2,128)S(1)} %pad_maximum_fusion.7), channel_id=1, replica_groups=mesh['dp'=8,'tensor'=4] {'dp','tensor'}, use_global_device_ids=true, to_apply=%region_44.45 | all-reduce | flops 1024 | bytes 8192 | tf_op jit(solution)/shard_map/psum | solution.py:72
  831.0 16.8 fusion.125
  847.8 41.0 %psum.108 = f32[2,512]{1,0:T(2,128)S(1)} all-reduce(f32[2,512]{1,0:T(2,128)S(1)} %pad_maximum_fusion.8), channel_id=1, replica_groups=mesh['dp'=8,'tensor'=4] {'dp','tensor'}, use_global_device_ids=true, to_apply=%region_47.48 | all-reduce | flops 1024 | bytes 8192 | tf_op jit(solution)/shard_map/psum | solution.py:72
  892.6 47.0 %all-gather.27.cloned.1.call-done = f32[49,64,512]{2,1,0:T(8,128)} async-done(((f32[49,16,512]{2,1,0:T(8,128)}), f32[49,64,512]{2,1,0:T(8,128)}) %all-gather.27.cloned.1.call-update) | async-done | bytes 6422544 | tf_op jit(solution)/shard_map/all_gather | solution.py:82
  939.7 16.2 fusion.122
  955.9 21.4 %psum.109 = f32[2,512]{1,0:T(2,128)S(1)} all-reduce(f32[2,512]{1,0:T(2,128)S(1)} %pad_maximum_fusion.9), channel_id=1, replica_groups=mesh['dp'=8,'tensor'=4] {'dp'}, use_global_device_ids=true, to_apply=%region_50.51 | all-reduce | flops 1024 | bytes 8192 | tf_op jit(solution)/shard_map/psum | solution.py:72
  986.4 7.2 fusion.158
  996.9 52.5 %reduce-scatter.13.cloned.1.call-done = f32[49,16,512]{2,1,0:T(8,128)} async-done(((f32[49,64,512]{2,1,0:T(8,128)}), f32[49,16,512]{2,1,0:T(8,128)}) %reduce-scatter.13.cloned.1.call-update) | async-done | bytes 1605648 | tf_op jit(solution)/shard_map/reduce_scatter | solution.py:78
  1051.3 39.4 %psum.110 = f32[2,512]{1,0:T(2,128)S(1)} all-reduce(f32[2,512]{1,0:T(2,128)S(1)} %pad_maximum_fusion.10), channel_id=1, replica_groups=mesh['dp'=8,'tensor'=4] {'dp','tensor'}, use_global_device_ids=true, to_apply=%region_54.55 | all-reduce | flops 1024 | bytes 8192 | tf_op jit(solution)/shard_map/psum | solution.py:72
  1143.4 42.7 %all-reduce.27 = (f32[2,512]{1,0:T(2,128)S(1)}, f32[9,32]{1,0:T(8,128)}) all-reduce(f32[2,512]{1,0:T(2,128)S(1)} %pad_maximum_fusion.11, f32[9,32]{1,0:T(8,128)S(1)} %multiply_reduce_fusion.21), channel_id=1, replica_groups=mesh['dp'=8,'tensor'=4] {'dp','tensor'}, use_global_device_ids=true, to_apply=%region_58.59 | all-reduce | flops 1312 | bytes 10496 | tf_op jit(solution)/shard_map/psum | solution.py:72
  1189.9 12.9 convolution_bitcast_fusion
  1216.3 7.7 fusion.160
  1228.2 7.6 fusion.159
  1235.9 7.8 fusion.10
  1270.3 7.8 fusion.3
  1278.1 18.1 %all-to-all-done.6 = f32[512,4,128]{0,2,1:T(8,128)} async-done(((f32[512,4,128]{0,2,1:T(8,128)}), f32[512,4,128]{0,2,1:T(8,128)}, u32[]{:S(2)}, u32[]{:S(2)}) %all-to-all-start.6) | async-done | bytes 1048608 | tf_op jit(solution)/shard_map/all_to_all | solution.py:134
  1310.6 15.9 all-to-all-done.4
  1329.0 16.4 reduce-scatter.17.cloned.1.call-done
  1345.4 36.1 %reduce-scatter.15.cloned.1.call-done = f32[1,1152,128]{2,1,0:T(8,128)} async-done(((f32[4,1152,128]{2,1,0:T(8,128)}), f32[1,1152,128]{2,1,0:T(8,128)}) %reduce-scatter.15.cloned.1.call-update) | async-done | bytes 589840 | tf_op jit(solution)/shard_map/reduce_scatter | solution.py:259
  1381.7 10.3 maximum_multiply_fusion
  1392.0 117.3 %all-reduce.32.cloned.1.call-done = f32[68,512]{1,0:T(8,128)} async-done(((f32[68,512]{1,0:T(8,128)}), f32[68,512]{1,0:T(8,128)}) %all-reduce.32.cloned.1.call-update) | async-done | bytes 139280 | tf_op jit(solution)/shard_map/psum | solution.py:264
  1512.2 20.6 %bitcast_add_fusion = f32[64,49,512]{2,0,1:T(8,128)} fusion(f32[49,64,512]{2,1,0:T(8,128)} %get-tuple-element.354, f32[64,49,512]{2,0,1:T(8,128)} %param.52, f32[49,64,512]{2,1,0:T(8,128)} %copy-done.1, f32[512]{0:T(512)S(1)} %copy-done.117, f32[512]{0:T(512)S(1)} %copy-done.95, f32[512]{0:T(512)S(1)} %copy-done.90, f32[512]{0:T(512)S(1)} %copy-done.101, ...), kind=kOutput, calls=%fused_computation.4 | convolution fusion | flops 4963008512 | bytes 46022912 | tf_op jit(solution)/shard_map/dot_general | solution.py:32
  1532.8 225.4 %all-reduce.34.cloned.1.call-done = (f32[2048,128]{1,0:T(8,128)}, f32[1,1152,128]{2,1,0:T(8,128)}, f32[128,2048]{1,0:T(8,128)}, f32[2048,128]{1,0:T(8,128)}, f32[4608,128]{1,0:T(8,128)}, /*index=5*/f32[128,2048]{1,0:T(8,128)}) async-done(((f32[2048,128]{1,0:T(8,128)}, f32[1,1152,128]{2,1,0:T(8,128)}, f32[128,2048]{1,0:T(8,128)}, f32[2048,128]{1,0:T(8,128)}, f32[4608,128]{1,0:T(8,128)}, ...) | async-done | bytes 7143440 | tf_op jit(solution)/shard_map/psum | solution.py:260
  (740 shorter events, 300.5 us)
Async XLA Ops:
  7.2 95.9 %reduce-scatter.7.cloned.1.call-start = ((), (), s32[]{:S(2)}) async-start(), calls=%async_computation.14 | async-start | bytes 8028160 | tf_op jit(solution)/shard_map/reduce_scatter | solution.py:78
  41.8 135.0 %all-gather.19.cloned.1.call-start = ((), (), s32[]{:S(2)}) async-start(), calls=%async_computation.15 | async-start | bytes 2949120 | tf_op jit(solution)/shard_map/all_gather | solution.py:150
  42.6 274.0 %all-gather.21.cloned.1.call-start = ((), (), s32[]{:S(2)}) async-start(), calls=%async_computation.16 | async-start | bytes 8028160 | tf_op jit(solution)/shard_map/all_gather | solution.py:82
  69.2 88.6 %copy-start.108 = (f32[49,32]{1,0:T(8,128)}, f32[49,32]{1,0:T(8,128)S(1)}, u32[]{:S(2)}) copy-start(f32[49,32]{1,0:T(8,128)S(1)} %copy.139) | copy-start | bytes 18820
  75.7 87.7 %copy-start.82 = (f32[76,512]{1,0:T(8,128)}, f32[76,512]{1,0:T(8,128)S(1)}, u32[]{:S(2)}) copy-start(f32[76,512]{1,0:T(8,128)S(1)} %all_gather.57) | copy-start | bytes 466948
  75.8 82.0 %copy-start.102 = (f32[1,512]{1,0:T(1,128)}, f32[1,512]{1,0:T(1,128)S(1)}, u32[]{:S(2)}) copy-start(f32[1,512]{1,0:T(1,128)S(1)} %get-tuple-element.304) | copy-start | bytes 6148
  75.8 82.0 %copy-start.118 = (f32[1,512]{1,0:T(1,128)}, f32[1,512]{1,0:T(1,128)S(1)}, u32[]{:S(2)}) copy-start(f32[1,512]{1,0:T(1,128)S(1)} %get-tuple-element.303) | copy-start | bytes 6148
  154.0 3.0 collective-permute-start
  157.8 5.8 collective-permute-start.1
  162.0 3.6 collective-permute-start.2
  251.3 29.2 %all-to-all-start.2 = ((f32[4,512,128]{2,1,0:T(8,128)}), f32[4,512,128]{2,1,0:T(8,128)S(1)}, u32[]{:S(2)}, u32[]{:S(2)}) async-start(f32[4,512,128]{2,1,0:T(8,128)} %bitcast.94), calls=%async_computation.3 | async-start | bytes 2097152 | tf_op jit(solution)/shard_map/all_to_all | solution.py:133
  280.5 29.5 %all-to-all-start.1 = ((f32[128,4,512]{2,0,1:T(8,128)}), f32[128,4,512]{2,0,1:T(8,128)S(1)}, u32[]{:S(2)}, u32[]{:S(2)}) async-start(f32[128,4,512]{2,0,1:T(8,128)} %bitcast.497), calls=%async_computation.2 | async-start | bytes 2097152 | tf_op jit(solution)/shard_map/all_to_all | solution.py:134
  284.0 154.7 %reduce-scatter.9.cloned.1.call-start = ((), (), s32[]{:S(2)}) async-start(), calls=%async_computation.17 | async-start | bytes 8028160 | tf_op jit(solution)/shard_map/reduce_scatter | solution.py:78
  285.3 83.4 %copy-start.28 = (f32[512,512,1]{1,0,2:T(8,128)}, f32[512,512,1]{1,0,2:T(8,128)S(1)}, u32[]{:S(2)}) copy-start(f32[512,512,1]{1,0,2:T(8,128)S(1)} %reshape.751) | copy-start | bytes 3145732
  363.5 613.9 %copy-start.85 = (f32[512]{0:T(512)}, f32[512]{0:T(512)S(1)}, u32[]{:S(2)}) copy-start(f32[512]{0:T(512)S(1)} %broadcast_divide_fusion.5) | copy-start | bytes 6148
  364.2 613.2 %copy-start.87 = (f32[512]{0:T(512)}, f32[512]{0:T(512)S(1)}, u32[]{:S(2)}) copy-start(f32[512]{0:T(512)S(1)} %get-tuple-element.158) | copy-start | bytes 6148
  383.0 124.8 %all-gather.23.cloned.1.call-start = ((), (), s32[]{:S(2)}) async-start(), calls=%async_computation.18 | async-start | bytes 11796480 | tf_op jit(solution)/shard_map/all_gather | solution.py:149
  383.6 249.8 %all-gather.25.cloned.1.call-start = ((), (), s32[]{:S(2)}) async-start(), calls=%async_computation.19 | async-start | bytes 8028160 | tf_op jit(solution)/shard_map/all_gather | solution.py:82
  578.8 197.7 %reduce-scatter.11.cloned.1.call-start = ((), (), s32[]{:S(2)}) async-start(), calls=%async_computation.20 | async-start | bytes 8028160 | tf_op jit(solution)/shard_map/reduce_scatter | solution.py:78
  719.3 220.3 %all-gather.27.cloned.1.call-start = ((), (), s32[]{:S(2)}) async-start(), calls=%async_computation.21 | async-start | bytes 8028160 | tf_op jit(solution)/shard_map/all_gather | solution.py:82
  847.8 91.9 %copy-start.29 = (f32[512,512,1]{1,0,2:T(8,128)S(1)}, f32[512,512,1]{1,0,2:T(8,128)}, u32[]{:S(2)}) copy-start(f32[512,512,1]{1,0,2:T(8,128)} %copy-done.28) | copy-start | bytes 3145732
  892.6 156.8 %reduce-scatter.13.cloned.1.call-start = ((), (), s32[]{:S(2)}) async-start(), calls=%async_computation.22 | async-start | bytes 8028160 | tf_op jit(solution)/shard_map/reduce_scatter | solution.py:78
  993.6 276.7 %all-gather.29.cloned.1.call-start = ((), (), s32[]{:S(2)}) async-start(), calls=%async_computation.23 | async-start | bytes 8028160 | tf_op jit(solution)/shard_map/all_gather | solution.py:82
  1094.6 14.3 collective-permute-start.3
  1096.1 12.8 collective-permute-start.4
  1132.2 6.3 collective-permute-start.5
  1189.8 155.6 %reduce-scatter.17.cloned.1.call-start = ((), (), s32[]{:S(2)}) async-start(), calls=%async_computation.26 | async-start | bytes 11796480 | tf_op jit(solution)/shard_map/reduce_scatter | solution.py:258
  1202.8 178.7 %reduce-scatter.15.cloned.1.call-start = ((), (), s32[]{:S(2)}) async-start(), calls=%async_computation.25 | async-start | bytes 2949120 | tf_op jit(solution)/shard_map/reduce_scatter | solution.py:259
  1224.0 23.0 %all-to-all-start.7 = ((f32[4,128,512]{2,1,0:T(8,128)}), f32[4,128,512]{2,1,0:T(8,128)}, u32[]{:S(2)}, u32[]{:S(2)}) async-start(f32[4,128,512]{2,1,0:T(8,128)} %bitcast.268), calls=%async_computation.13 | async-start | bytes 2097152 | tf_op jit(solution)/shard_map/all_to_all | solution.py:133
  1247.0 18.9 %all-to-all-start.5 = ((f32[4,128,512]{2,1,0:T(8,128)}), f32[4,128,512]{2,1,0:T(8,128)}, u32[]{:S(2)}, u32[]{:S(2)}) async-start(f32[4,128,512]{2,1,0:T(8,128)} %bitcast.558), calls=%async_computation.10 | async-start | bytes 2097152 | tf_op jit(solution)/shard_map/all_to_all | solution.py:133
  1265.8 30.3 %all-to-all-start.6 = ((f32[512,4,128]{0,2,1:T(8,128)}), f32[512,4,128]{0,2,1:T(8,128)}, u32[]{:S(2)}, u32[]{:S(2)}) async-start(f32[512,4,128]{0,2,1:T(8,128)} %bitcast.557), calls=%async_computation.11 | async-start | bytes 2097152 | tf_op jit(solution)/shard_map/all_to_all | solution.py:134
  1296.2 30.3 %all-to-all-start.4 = ((f32[512,4,128]{0,2,1:T(8,128)}), f32[512,4,128]{0,2,1:T(8,128)}, u32[]{:S(2)}, u32[]{:S(2)}) async-start(f32[512,4,128]{0,2,1:T(8,128)} %bitcast.553), calls=%async_computation.8 | async-start | bytes 2097152 | tf_op jit(solution)/shard_map/all_to_all | solution.py:134
  1300.4 208.9 %all-reduce.32.cloned.1.call-start = ((), (), s32[]{:S(2)}) async-start(), calls=%async_computation.24 | async-start | bytes 294912 | tf_op jit(solution)/shard_map/psum | solution.py:264
  1303.3 454.9 %all-reduce.34.cloned.1.call-start = ((), (), s32[]{:S(2)}) async-start(), calls=%async_computation.27 | async-start | bytes 14286848 | tf_op jit(solution)/shard_map/psum | solution.py:260
  1308.0 73.5 %copy-start.88 = (f32[512]{0:T(512)S(1)}, f32[512]{0:T(512)}, u32[]{:S(2)}) copy-start(f32[512]{0:T(512)} %copy-done.87) | copy-start | bytes 6148
  1308.0 73.5 %copy-start.90 = (f32[512]{0:T(512)S(1)}, f32[512]{0:T(512)}, u32[]{:S(2)}) copy-start(f32[512]{0:T(512)} %copy-done.89) | copy-start | bytes 6148
  1308.0 73.5 %copy-start.95 = (f32[512]{0:T(512)S(1)}, f32[512]{0:T(512)}, u32[]{:S(2)}) copy-start(f32[512]{0:T(512)} %copy-done.94) | copy-start | bytes 6148
  1308.0 73.5 %copy-start.99 = (f32[512]{0:T(512)S(1)}, f32[512]{0:T(512)}, u32[]{:S(2)}) copy-start(f32[512]{0:T(512)} %param.41) | copy-start | bytes 6148
  1308.1 73.5 %copy-start.101 = (f32[512]{0:T(512)S(1)}, f32[512]{0:T(512)}, u32[]{:S(2)}) copy-start(f32[512]{0:T(512)} %param.50) | copy-start | bytes 6148
  1308.1 73.5 %copy-start.115 = (f32[512]{0:T(512)S(1)}, f32[512]{0:T(512)}, u32[]{:S(2)}) copy-start(f32[512]{0:T(512)} %param.42) | copy-start | bytes 6148
  1308.1 73.5 %copy-start.117 = (f32[512]{0:T(512)S(1)}, f32[512]{0:T(512)}, u32[]{:S(2)}) copy-start(f32[512]{0:T(512)} %param.51) | copy-start | bytes 6148
  1381.6 127.7 %copy-start.111 = (f32[1,512]{1,0:T(1,128)S(1)}, f32[1,512]{1,0:T(1,128)}, u32[]{:S(2)}) copy-start(f32[1,512]{1,0:T(1,128)} %copy-done.110) | copy-start | bytes 6148
  1381.6 127.7 %copy-start.113 = (f32[1,512]{1,0:T(1,128)S(1)}, f32[1,512]{1,0:T(1,128)}, u32[]{:S(2)}) copy-start(f32[1,512]{1,0:T(1,128)} %copy-done.112) | copy-start | bytes 6148
  1381.6 127.7 %copy-start.121 = (f32[1,512]{1,0:T(1,128)S(1)}, f32[1,512]{1,0:T(1,128)}, u32[]{:S(2)}) copy-start(f32[1,512]{1,0:T(1,128)} %copy-done.120) | copy-start | bytes 6148
  1381.6 127.7 %copy-start.123 = (f32[1,512]{1,0:T(1,128)S(1)}, f32[1,512]{1,0:T(1,128)}, u32[]{:S(2)}) copy-start(f32[1,512]{1,0:T(1,128)} %copy-done.122) | copy-start | bytes 6148
  1381.6 127.7 %copy-start.125 = (f32[1,512]{1,0:T(1,128)S(1)}, f32[1,512]{1,0:T(1,128)}, u32[]{:S(2)}) copy-start(f32[1,512]{1,0:T(1,128)} %copy-done.124) | copy-start | bytes 6148
  1381.7 127.7 %copy-start.127 = (f32[1,512]{1,0:T(1,128)S(1)}, f32[1,512]{1,0:T(1,128)}, u32[]{:S(2)}) copy-start(f32[1,512]{1,0:T(1,128)} %copy-done.126) | copy-start | bytes 6148
  1381.7 130.5 %copy-start.25 = (f32[512,512,1]{1,0,2:T(8,128)S(1)}, f32[512,512,1]{1,0,2:T(8,128)}, u32[]{:S(2)}) copy-start(f32[512,512,1]{1,0,2:T(8,128)} %copy-done.24) | copy-start | bytes 3145732
  (177 other events, 3150.0 us)
Sparse Core Ops, SparseCore 0:
  41.9 61.1 reduce-scatter.6
  104.8 25.2 all-gather.18
  251.4 65.1 all-gather.20
  383.2 55.5 reduce-scatter.8
  440.2 67.5 all-gather.22
  579.0 54.4 all-gather.24
  719.4 57.0 reduce-scatter.10
  892.7 46.9 all-gather.26
  993.8 55.5 reduce-scatter.12
  1190.0 51.4 all-gather.28
  1244.0 101.3 reduce-scatter.16
  1348.4 33.0 reduce-scatter.14
  1388.5 120.7 all-reduce.31
  1516.3 241.8 all-reduce.33

commit v2 on v1

--- a/solution.py
+++ b/solution.py
@@ -1,7 +1,11 @@
+import functools
+
 import jax
 import jax.numpy as jnp
 import numpy as np
 from jax import lax
+from jax.experimental import pallas as pl
+from jax.experimental.pallas import tpu as pltpu
 from jax.sharding import PartitionSpec as P
 
 SIDE = 7
@@ -54,32 +58,349 @@
     return weight.reshape(9, chans, outs)[::-1].transpose(0, 2, 1).reshape(9 * outs, chans)
 
 
-def moments(h, mask, count, axes):
-    local = jnp.sum(mask) * CELLS
-    total = jnp.sum(h * mask, axis=(0, 1))
-    mean = total / jnp.maximum(local, 1.0)
+MESH = pl.DeviceIdType.MESH
+ROWS = 7
+CHUNKS = CELLS // ROWS
+HBM = pl.BlockSpec(memory_space=pl.ANY)
+VMEM = pl.BlockSpec(memory_space=pltpu.VMEM)
+SMEM = pl.BlockSpec(memory_space=pltpu.SMEM)
+
+
+def shape(*dims):
+    return jax.ShapeDtypeStruct(dims, jnp.float32)
+
+
+def params(number, megabytes):
+    return pltpu.CompilerParams(collective_id=number, has_side_effects=True, vmem_limit_bytes=megabytes << 20)
+
+
+class Group:
+    def __init__(self, dp, tensor, whole):
+        self.tensor = tensor
+        self.whole = whole
+        self.size = dp * tensor if whole else dp
+        across, along = lax.axis_index("dp"), lax.axis_index("tensor")
+        self.me = across * tensor + along if whole else across
+
+    def device(self, flat):
+        if self.whole:
+            return {"dp": flat // self.tensor, "tensor": flat % self.tensor}
+        return {"dp": flat}
+
+    def others(self, act):
+        def step(index, carry):
+            act(self.device((self.me + index) % self.size))
+            return carry
+
+        lax.fori_loop(1, self.size, step, 0)
+
+    def greet(self):
+        barrier = pltpu.get_barrier_semaphore()
+        self.others(lambda device: pl.semaphore_signal(barrier, 1, device_id=device, device_id_type=MESH))
+        return barrier
+
+    def meet(self, barrier):
+        pl.semaphore_wait(barrier, self.size - 1)
+
+    def exchange(self, note, box, sems):
+        box[self.me] = note[...]
+        self.others(
+            lambda device: pltpu.make_async_remote_copy(
+                src_ref=note, dst_ref=box.at[self.me], send_sem=sems.at[0], recv_sem=sems.at[1],
+                device_id=device, device_id_type=MESH,
+            ).start()
+        )
+        bulk = box.at[pl.ds(0, self.size - 1)]
+        pltpu.make_async_copy(bulk, bulk, sems.at[1]).wait()
+        pltpu.make_async_copy(bulk, bulk, sems.at[0]).wait()
+
+
+def to_tile(note, first, second):
+    for index in range(4):
+        lanes = slice(index * 128, (index + 1) * 128)
+        note[index : index + 1] = first[:, lanes]
+        note[index + 4 : index + 5] = second[:, lanes]
+
+
+def to_row(tile):
+    return jnp.concatenate([tile[index : index + 1] for index in range(4)], axis=1)
+
+
+def combine_moments(box, counts, size):
+    total = counts[size]
+    first = lax.fori_loop(0, size, lambda i, acc: acc + counts[i] * box[i], jnp.zeros((8, 128), jnp.float32))
+    mean = first / total
+
+    def step(i, acc):
+        spread = box[i] - mean
+        return acc[0] + box[i], acc[1] + counts[i] * spread * spread
+
+    zero = jnp.zeros((8, 128), jnp.float32)
+    inner, outer_part = lax.fori_loop(0, size, step, (zero, zero))
+    var = (inner[4:8] + outer_part[0:4]) / total
+    return mean[0:4], lax.rsqrt(var + EPS)
+
+
+def positions(body, init):
+    return lax.fori_loop(0, CELLS, body, init)
+
+
+def scatter_frames(p, h, pair, cross, arrived, sems, along, own):
+    mate, far = along + 1 - 2 * (along % 2), (along + 2) % 4
+    far_mate = (mate + 2) % 4
+    local, send_1, recv_1, send_2, recv_2 = sems
+
+    def frames(device):
+        return pl.ds(pl.multiple_of(device * own, own), own)
+
+    def cut(k):
+        return pl.ds(k * ROWS, ROWS)
+
+    pairs = []
+    for part, owner in ((0, far_mate), (1, mate)):
+        row = []
+        for k in range(CHUNKS):
+            copy = pltpu.make_async_remote_copy(
+                src_ref=p.at[cut(k), frames(owner)], dst_ref=pair.at[part, cut(k)], send_sem=send_1.at[part, k],
+                recv_sem=recv_1.at[part, k], device_id={"tensor": mate}, device_id_type=MESH,
+            )
+            copy.start()
+            row.append(copy)
+        pairs.append(row)
+    loads = []
+    for part, (owner, target) in enumerate(((far, cross), (along, h))):
+        copy = pltpu.make_async_copy(p.at[:, frames(owner)], target, local.at[part])
+        copy.start()
+        loads.append(copy)
+    sends = [
+        pltpu.make_async_remote_copy(
+            src_ref=cross.at[cut(k)], dst_ref=arrived.at[cut(k)], send_sem=send_2.at[k], recv_sem=recv_2.at[k],
+            device_id={"tensor": far}, device_id_type=MESH,
+        )
+        for k in range(CHUNKS)
+    ]
+    loads[0].wait()
+    for k in range(CHUNKS):
+        pairs[0][k].wait_recv()
+        cross[cut(k)] = cross[cut(k)] + pair[0, cut(k)]
+        if k:
+            sends[k - 1].start()
+    loads[1].wait()
+    for k in range(CHUNKS):
+        pairs[1][k].wait_recv()
+        h[cut(k)] = h[cut(k)] + pair[1, cut(k)]
+        if k == 0:
+            sends[CHUNKS - 1].start()
+    for k in range(CHUNKS):
+        sends[k].wait_recv()
+        h[cut(k)] = h[cut(k)] + arrived[cut(k)]
+    for k in range(CHUNKS):
+        sends[k].wait_send()
+        pairs[0][k].wait_send()
+        pairs[1][k].wait_send()
+
+
+def gather_frames(fill, act, out, sems, along, own):
+    mate, far = along + 1 - 2 * (along % 2), (along + 2) % 4
+    local, send_1, recv_1, send_2, recv_2, send_3, recv_3 = sems
+
+    def place(device, k):
+        return out.at[pl.ds(k * ROWS, ROWS), pl.ds(pl.multiple_of(device * own, own), own)]
+
+    def remote(src, dst, send, recv, device):
+        return pltpu.make_async_remote_copy(
+            src_ref=src, dst_ref=dst, send_sem=send, recv_sem=recv, device_id={"tensor": device}, device_id_type=MESH
+        )
+
+    def chunk(k):
+        return act.at[pl.ds(k * ROWS, ROWS)]
+
+    near = [remote(chunk(k), place(along, k), send_1.at[k], recv_1.at[k], mate) for k in range(CHUNKS)]
+    over = [remote(chunk(k), place(along, k), send_2.at[k], recv_2.at[k], far) for k in range(CHUNKS)]
+    pass_on = [remote(place(far, k), place(far, k), send_3.at[k], recv_3.at[k], mate) for k in range(CHUNKS)]
+    kept = [pltpu.make_async_copy(chunk(k), place(along, k), local.at[k]) for k in range(CHUNKS)]
+
+    def launch(k):
+        over[k].start()
+        near[k].start()
+        kept[k].start()
+
+    for k in range(CHUNKS):
+        fill(k)
+        if k:
+            launch(k - 1)
+    launch(CHUNKS - 1)
+    for k in range(CHUNKS):
+        over[k].wait_recv()
+        pass_on[k].start()
+    for k in range(CHUNKS):
+        near[k].wait()
+        over[k].wait_send()
+        pass_on[k].wait()
+        kept[k].wait()
+
+
+SCATTER_SEMS = [pltpu.SemaphoreType.DMA((2,))] + [pltpu.SemaphoreType.DMA((2, CHUNKS))] * 2 + [pltpu.SemaphoreType.DMA((CHUNKS,))] * 2
+GATHER_SEMS = [pltpu.SemaphoreType.DMA((CHUNKS,))] * 7
+
+
+def forward_kernel(dp, tensor, own, scatter, gather, x, counts, mask, gain, bias, xhat, rstd, act, *scratch):
+    group = Group(dp, tensor, True)
+    along = lax.axis_index("tensor")
+    scratch = list(scratch)
+    note, box, sems = scratch[:3]
+    scratch = scratch[3:]
+    barrier = group.greet()
+    h = x
+    if scatter:
+        h, pair, cross, arrived = scratch[:4]
+        group.meet(barrier)
+        scatter_frames(x, h, pair, cross, arrived, scratch[4:9], along, own)
+        scratch = scratch[9:]
+    keep = mask[...]
+    zero = jnp.zeros(keep.shape, jnp.float32)
+    mine = counts[group.me]
+    mean = jnp.sum(positions(lambda i, acc: acc + h[i], zero) * keep, axis=0, keepdims=True) / jnp.maximum(mine, 1.0)
+
+    def square(i, acc):
+        off = h[i] - mean
+        return acc + off * off
+
+    second = jnp.sum(positions(square, zero) * keep, axis=0, keepdims=True)
+    to_tile(note, mean, second)
+    if not scatter:
+        group.meet(barrier)
+    group.exchange(note, box, sems)
+    mean, scale = combine_moments(box, counts, group.size)
+    mean, scale = to_row(mean), to_row(scale)
+    rstd[...] = scale
+    gains, biases = gain[...], bias[...]
+    spread = scratch[0] if gather else act
+
+    def finish(i, carry):
+        normed = (h[i] - mean) * scale
+        xhat[i] = normed
+        spread[i] = jnp.maximum(gains * normed + biases, 0.0)
+        return carry
+
+    if gather:
+        fill = lambda k: lax.fori_loop(k * ROWS, (k + 1) * ROWS, finish, 0)
+        gather_frames(fill, spread, act, scratch[1:8], along, own)
+    else:
+        positions(finish, 0)
+
+
+def backward_kernel(dp, tensor, own, scatter, gather, x, counts, mask, gain, bias, rstd, xhat, sums, back, *scratch):
+    group = Group(dp, tensor, True)
+    along = lax.axis_index("tensor")
+    scratch = list(scratch)
+    note, box, sems = scratch[:3]
+    scratch = scratch[3:]
+    barrier = group.greet()
+    d = x
+    if scatter:
+        d, pair, cross, arrived = scratch[:4]
+        group.meet(barrier)
+        scatter_frames(x, d, pair, cross, arrived, scratch[4:9], along, own)
+        scratch = scratch[9:]
+    gains, biases = gain[...], bias[...]
+    zero = jnp.zeros(mask.shape, jnp.float32)
+
+    def through(i):
+        return jnp.where(gains * xhat[i] + biases > 0, d[i], 0.0)
+
+    def add(i, acc):
+        grad = through(i)
+        return acc[0] + grad, acc[1] + grad * xhat[i]
+
+    first, second = positions(add, (zero, zero))
+    to_tile(note, jnp.sum(first, axis=0, keepdims=True), jnp.sum(second, axis=0, keepdims=True))
+    if not scatter:
+        group.meet(barrier)
+    group.exchange(note, box, sems)
+    total = lax.fori_loop(0, group.size, lambda i, acc: acc + box[i], jnp.zeros((8, 128), jnp.float32))
+    sums[...] = total
+    shared = total / counts[group.size]
+    first, second = to_row(shared[0:4]), to_row(shared[4:8])
+    factor = gains * rstd[...]
+    keep = mask[...]
+    spread = scratch[0] if gather else back
+
+    def finish(i, carry):
+        spread[i] = factor * (through(i) - keep * (first + xhat[i] * second))
+        return carry
+
+    if gather:
+        fill = lambda k: lax.fori_loop(k * ROWS, (k + 1) * ROWS, finish, 0)
+        gather_frames(fill, spread, back, scratch[1:8], along, own)
+    else:
+        positions(finish, 0)
+
+
+def narrow_norm(number, mode, sizes, x, *operands, scatter=False, gather=False):
+    dp, tensor, frames, chans = sizes
+    own = frames // tensor
+    block = (CELLS, own, chans)
+    flat = dp * tensor
+    scratch = [pltpu.VMEM((8, 128), jnp.float32), pltpu.VMEM((flat, 8, 128), jnp.float32), pltpu.SemaphoreType.DMA((2,))]
+    if scatter:
+        scratch += [pltpu.VMEM(block, jnp.float32), pltpu.VMEM((2,) + block, jnp.float32)]
+        scratch += [pltpu.VMEM(block, jnp.float32)] * 2 + SCATTER_SEMS
+    if gather:
+        scratch += [pltpu.VMEM(block, jnp.float32)] + GATHER_SEMS
+    last = shape(CELLS, frames, chans) if gather else shape(*block)
+    if mode == "forward":
+        kernel, outs = forward_kernel, (shape(*block), shape(1, chans), last)
+    else:
+        kernel, outs = backward_kernel, (shape(8, 128), last)
+    return pl.pallas_call(
+        functools.partial(kernel, dp, tensor, own, scatter, gather),
+        out_shape=outs,
+        in_specs=[HBM if scatter else VMEM, SMEM] + [VMEM] * (len(operands) - 1),
+        out_specs=tuple([VMEM] * (len(outs) - 1) + [HBM if gather else VMEM]),
+        scratch_shapes=scratch,
+        compiler_params=params(number, 24),
+        name="narrow_" + mode,
+    )(x, *operands)
+
+
+def wide_kernel(dp, tensor, moments_mode, x, counts, out, box, sems):
+    group = Group(dp, tensor, False)
+    group.meet(group.greet())
+    group.exchange(x, box, sems)
+    if moments_mode:
+        mean, scale = combine_moments(box, counts, group.size)
+        out[0:4] = mean
+        out[4:8] = scale
+    else:
+        out[...] = lax.fori_loop(0, group.size, lambda i, acc: acc + box[i], jnp.zeros((8, 128), jnp.float32))
+
+
+def wide_exchange(number, sizes, counts, first, second, moments_mode):
+    dp, tensor = sizes[:2]
+    tile = jnp.concatenate([first.reshape(4, 128), second.reshape(4, 128)])
+    out = pl.pallas_call(
+        functools.partial(wide_kernel, dp, tensor, moments_mode),
+        out_shape=shape(8, 128),
+        in_specs=[VMEM, SMEM],
+        out_specs=VMEM,
+        scratch_shapes=[pltpu.VMEM((dp, 8, 128), jnp.float32), pltpu.SemaphoreType.DMA((2,))],
+        compiler_params=params(number, 4),
+        name="wide_exchange",
+    )(tile, counts)
+    return out[0:4].reshape(-1), out[4:8].reshape(-1)
+
+
+def wide_moments(number, sizes, counts, h, mask, here):
+    mean = jnp.sum(h * mask, axis=(0, 1)) / jnp.maximum(here, 1.0)
     second = jnp.sum(mask * (h - mean) ** 2, axis=(0, 1))
-    local_row = jnp.full_like(mean, local)
-    all_parts = lax.all_gather(jnp.stack([mean, second, local_row]), axes)
-    means, seconds, counts = all_parts[:, 0], all_parts[:, 1], all_parts[:, 2]
-    mean = jnp.sum(means * counts, axis=0) / count
-    var = (jnp.sum(seconds, axis=0) + jnp.sum(counts * (means - mean) ** 2, axis=0)) / count
-    return mean, lax.rsqrt(var + EPS)
-
-
-def norm_back(grad, xhat, mask, gain, rstd, count, axes):
-    sums = jnp.stack([jnp.sum(grad, axis=(0, 1)), jnp.sum(grad * xhat, axis=(0, 1))])
-    sums = lax.psum(sums, axes)
-    back = gain * rstd * (grad - mask * (sums[0] + xhat * sums[1]) / count)
-    return back, sums[1], sums[0]
-
-
-def reduce_frames(partial):
-    return lax.psum_scatter(partial, "tensor", scatter_dimension=1, tiled=True)
-
-
-def gather_frames(part):
-    return lax.all_gather(part, "tensor", axis=1, tiled=True)
+    return wide_exchange(number, sizes, counts, mean, second, True)
+
+
+def wide_back(number, sizes, counts, grad, xhat, mask, gain, rstd):
+    first, second = jnp.sum(grad, axis=(0, 1)), jnp.sum(grad * xhat, axis=(0, 1))
+    first, second = wide_exchange(number, sizes, counts, first, second, False)
+    return gain * rstd * (grad - mask * (first + xhat * second) / counts[sizes[0]]), second, first
 
 
 def shift_from(value, steps):
@@ -120,7 +441,12 @@
     seed = jnp.transpose(cotangent, (1, 0, 2))
 
     valid = (frame_clip >= 0).astype(jnp.float32)
-    count = lax.psum(jnp.sum(valid) * CELLS, "dp")
+    sizes = (lax.axis_size("dp"), tensor, frames, tensor * group_taps.shape[2])
+    parts = lax.all_gather(jnp.sum(valid.reshape(tensor, own), axis=1) * CELLS, "dp")
+    count = jnp.sum(parts)
+    counts = jnp.concatenate([parts.reshape(-1), count[None]])
+    wide_counts = jnp.concatenate([jnp.sum(parts, axis=1), count[None]])
+    here_count = jnp.sum(valid) * CELLS
     wide_mask = valid[None, :, None]
     padded = jnp.pad(frame_clip, (reach + 1, reach + 1), constant_values=-2)
     clips = lax.dynamic_slice(padded, (at * own,), (own + 2 * reach + 2,))
@@ -129,6 +455,7 @@
     prev_ext = ((here >= 0) & (clips[:-2] == here)).astype(jnp.float32)[None, :, None]
     mask = (here >= 0).astype(jnp.float32)[reach : reach + own][None, :, None]
     next_own = next_ext[0, reach : reach + own]
+    mask = jnp.broadcast_to(mask[0], (own, sizes[3]))
 
     rows = lambda w: lax.all_to_all(w, "tensor", 0, 1, tiled=True)
     cols = lambda w: lax.all_to_all(w, "tensor", 1, 0, tiled=True)
@@ -144,16 +471,13 @@
     )
     small = lax.all_gather(small, "tensor", axis=1, tiled=True)
     md, mu = small[:rank].T, small[rank : 2 * rank]
-    mb, g_red, b_red, g_grp, b_grp, g_nar, b_nar, g_spa, b_spa = [small[2 * rank + i] for i in range(9)]
+    mb, g_red, b_red, g_grp, b_grp, g_nar, b_nar, g_spa, b_spa = [small[2 * rank + i : 2 * rank + i + 1] for i in range(9)]
     taps = small[2 * rank + 9 : 2 * rank + 12]
     spatial = lax.all_gather(spatial_second, "tensor", axis=1, tiled=True)
     group_w = lax.all_gather(group_spatial, "tensor", axis=0, tiled=True)
 
-    h1 = reduce_frames(mm(x, w_reduce, FWD))
-    mean1, r1 = moments(h1, mask, count, BOTH)
-    xh1 = (h1 - mean1) * r1
-    n1 = g_red * xh1 + b_red
-    act1 = jnp.maximum(n1, 0.0)
+    p1 = mm(x, w_reduce, FWD)
+    xh1, r1, act1 = narrow_norm(0, "forward", sizes, p1, counts, mask, g_red, b_red, scatter=True)
 
     edges = jnp.asarray(edge_mask())
     w_pos = jnp.sum(edges[:, :, None] * motion_kernel[None], axis=1)
@@ -178,48 +502,37 @@
         mids.append(stacked[:, mine])
         outs.append(carry[:, mine])
     grouped = jnp.concatenate(outs, axis=-1)
-    mean2, r2 = moments(grouped, mask, count, BOTH)
-    xh2 = (grouped - mean2) * r2
-    n2 = g_grp * xh2 + b_grp
-    mixed = gather_frames(jnp.maximum(n2, 0.0))
+    xh2, r2, mixed = narrow_norm(1, "forward", sizes, grouped, counts, mask, g_grp, b_grp, gather=True)
     h3 = mm(mixed, w_expand, FWD)
-    mean3, r3 = moments(h3, wide_mask, count, "dp")
+    mean3, r3 = wide_moments(2, sizes, wide_counts, h3, wide_mask, here_count)
     xh3 = (h3 - mean3) * r3
     pre3 = gain_expand * xh3 + bias_expand + x
     middle = jnp.maximum(pre3, 0.0)
 
-    h4 = reduce_frames(mm(middle, w_reduce2, FWD))
-    mean4, r4 = moments(h4, mask, count, BOTH)
-    xh4 = (h4 - mean4) * r4
-    n4 = g_nar * xh4 + b_nar
-    stacked4 = stack9(jnp.maximum(n4, 0.0))
+    p4 = mm(middle, w_reduce2, FWD)
+    xh4, r4, act4 = narrow_norm(3, "forward", sizes, p4, counts, mask, g_nar, b_nar, scatter=True)
+    stacked4 = stack9(act4)
     h5 = mm(stacked4, spatial, FWD)
-    mean5, r5 = moments(h5, mask, count, BOTH)
-    xh5 = (h5 - mean5) * r5
-    n5 = g_spa * xh5 + b_spa
-    conv_act = gather_frames(jnp.maximum(n5, 0.0))
+    xh5, r5, conv_act = narrow_norm(4, "forward", sizes, h5, counts, mask, g_spa, b_spa, gather=True)
     h6 = mm(conv_act, w_expand2, FWD)
-    mean6, r6 = moments(h6, wide_mask, count, "dp")
+    mean6, r6 = wide_moments(5, sizes, wide_counts, h6, wide_mask, here_count)
     xh6 = (h6 - mean6) * r6
     pre6 = gain_output * xh6 + bias_output + middle
     output = wide_mask * jnp.maximum(pre6, 0.0)
 
     d_last = jnp.where(pre6 > 0, seed * wide_mask, 0.0)
-    d6, gg_output, gb_output = norm_back(d_last, xh6, wide_mask, gain_output, r6, count, "dp")
+    d6, gg_output, gb_output = wide_back(6, sizes, wide_counts, d_last, xh6, wide_mask, gain_output, r6)
     gw_expand2 = outer(conv_act, d6, GRAD)
-    d_n5 = jnp.where(n5 > 0, reduce_frames(mm_t(d6, w_expand2, BWD)), 0.0)
-    d5, gg_spa, gb_spa = norm_back(d_n5, xh5, mask, g_spa, r5, count, BOTH)
+    s5, d5 = narrow_norm(7, "backward", sizes, mm_t(d6, w_expand2, BWD), counts, mask, g_spa, b_spa, r5, xh5, scatter=True)
     gw_spatial = outer(stacked4, d5, GRAD)
-    d_n4 = jnp.where(n4 > 0, mm(stack9(d5), flip_taps(spatial, d5.shape[2]), BWD), 0.0)
-    d4, gg_nar, gb_nar = norm_back(d_n4, xh4, mask, g_nar, r4, count, BOTH)
-    d4_all = gather_frames(d4) * wide_mask
+    d_act4 = mm(stack9(d5), flip_taps(spatial, d5.shape[2]), BWD)
+    s4, d4_all = narrow_norm(8, "backward", sizes, d_act4, counts, mask, g_nar, b_nar, r4, xh4, gather=True)
     gw_reduce2 = outer(middle, d4_all, GRAD)
     d_pre3 = jnp.where(pre3 > 0, d_last + mm_t(d4_all, w_reduce2, BWD), 0.0)
 
-    d3, gg_expand, gb_expand = norm_back(d_pre3, xh3, wide_mask, gain_expand, r3, count, "dp")
+    d3, gg_expand, gb_expand = wide_back(9, sizes, wide_counts, d_pre3, xh3, wide_mask, gain_expand, r3)
     gw_expand = outer(mixed, d3, GRAD)
-    d_n2 = jnp.where(n2 > 0, reduce_frames(mm_t(d3, w_expand, BWD)), 0.0)
-    d2, gg_grp, gb_grp = norm_back(d_n2, xh2, mask, g_grp, r2, count, BOTH)
+    s2, d2 = narrow_norm(10, "backward", sizes, mm_t(d3, w_expand, BWD), counts, mask, g_grp, b_grp, r2, xh2, scatter=True)
     d2_ext = halo(d2, reach)
     d_exc, gw_group, g_taps = [None] * groups, [None] * groups, [None] * groups
     carry = 0.0
@@ -249,9 +562,8 @@
     g_mk = jnp.sum(edges[:, :, None] * g_pos[:, None, :], axis=0)
     d_motion = w_pos[:, None, :] * d_ahead[None] - d_pool[None]
     g_md = outer(act1, d_motion, FWD)
-    d_n1 = jnp.where(n1 > 0, d_exc * gate[None] + mm_t(d_motion, md, FWD), 0.0)
-    d1, gg_red, gb_red = norm_back(d_n1, xh1, mask, g_red, r1, count, BOTH)
-    d1_all = gather_frames(d1) * wide_mask
+    d_act1 = d_exc * gate[None] + mm_t(d_motion, md, FWD)
+    s1, d1_all = narrow_norm(11, "backward", sizes, d_act1, counts, mask, g_red, b_red, r1, xh1, gather=True)
     gw_reduce = outer(x, d1_all, GRAD)
     grad_features = d_pre3 + mm_t(d1_all, w_reduce, BWD)
 
@@ -262,7 +574,8 @@
     )
     tiny = jnp.concatenate([g_md.T, g_mu, g_mb[None], jnp.concatenate(g_taps, axis=-1)], axis=0)
     tiny, g_mk = lax.psum((tiny, g_mk), BOTH)
-    narrow = jnp.stack([gg_red, gb_red, gg_grp, gb_grp, gg_nar, gb_nar, gg_spa, gb_spa])
+    pairs = [total.reshape(2, -1)[::-1] for total in (s1, s2, s4, s5)]
+    narrow = jnp.concatenate(pairs)
     tiny = lax.dynamic_slice(jnp.concatenate([tiny, narrow]), (0, at * gw), (2 * rank + 12, gw))
     vec = tiny[2 * rank + 4 :]
     return (

time: 1790 us -> 1380 us (0.77)
  Pallas kernels: 0 us -> 489 us
  waiting for transfers between devices: 745 us -> 302 us
  blocking collectives: 507 us -> 75.6 us
  other arithmetic: 96.5 us -> 62.7 us
    pallas_call x0 -> x12, Pallas kernels: none -> 489 us  [the longest x8 461 us: narrow_norm(): pl.pallas_call(functools.partial(kernel, dp, tensor, own, scatter, gather...]
    all_gather x6 -> x0, blocking collectives: 228 us -> none  [moments(): all_parts = lax.all_gather(jnp.stack([mean, second, local_row]), axes)]
    psum x7 -> x1, blocking collectives: 225 us -> 39.3 us  [local(): tiny, g_mk = lax.psum((tiny, g_mk), BOTH)]
    reduce_scatter x4 -> x0, waiting for transfers between devices: 172 us -> none  [reduce_frames(): return lax.psum_scatter(partial, 'tensor', scatter_dimension=1, tiled=True)]
    all_gather x4 -> x0, waiting for transfers between devices: 77.9 us -> none  [gather_frames(): return lax.all_gather(part, 'tensor', axis=1, tiled=True)]
    psum x1, waiting for transfers between devices: 117 us -> 41.3 us  [local(): tiny, g_mk = lax.psum((tiny, g_mk), BOTH)]
    all_to_all x3 -> x4, waiting for transfers between devices: 58.7 us -> 10.1 us  [local(): cols = lambda w: lax.all_to_all(w, 'tensor', 1, 0, tiled=True)]
    all_to_all x2 -> x0, blocking collectives: 47.6 us -> none  [the longest x1 29 us: local(): cols = lambda w: lax.all_to_all(w, 'tensor', 1, 0, tiled=True)]
  transfers between devices with their start and end apart: 26 -> 20, of which waited for: 21 -> 6; matrix products, arithmetic and copies ran while one was open for 11% -> 19% of each run, Pallas kernels for 0% -> 24%
where the time goes in v2:
time: 1380 us; the launch traced here: 1370 us
  Pallas kernels  489 us (35%)
  waiting for transfers between devices  302 us (22%)
  matrix products  241 us (17%)
  local copies, waits for them, and re-layouts  127 us (9%)
  blocking collectives  75.6 us (5%)
  other arithmetic  62.7 us (5%)
  starting transfers between devices  52.7 us (4%)
  between operations  19 us (1%)
    pallas_call x8, Pallas kernels, narrow_norm(): pl.pallas_call(functools.partial(kernel, dp, tensor, own, scatter, gather...  461 us
    psum x1, waiting for transfers between devices, local(): lax.psum((cols(gw_reduce), rows(gw_expand), cols(gw_reduce2), rows(gw_exp...  247 us
    dot_general x15, matrix products, mm(): lax.dot_general(values, weight, (((values.ndim - 1,), (0,)), ((), ())), p...  138 us
    unnamed x422, local copies, waits for them, and re-layouts  60.6 us
    dot_general x6, matrix products, mm_t(): lax.dot_general(values, weight, (((values.ndim - 1,), (1,)), ((), ())), p...  51.8 us
    dot_general x10, matrix products, outer(): lax.dot_general(left, right, (((0, 1), (0, 1)), ((), ())), precision=prec...  50.4 us
    psum x1, waiting for transfers between devices, local(): tiny, g_mk = lax.psum((tiny, g_mk), BOTH)  41.3 us
    psum x1, blocking collectives, local(): tiny, g_mk = lax.psum((tiny, g_mk), BOTH)  39.3 us
  transfers between devices with their start and end apart: 20, of which 6 were waited for; matrix products, arithmetic and copies ran while one was open for 19% of the time, Pallas kernels for 24%

profile of v2, /device:TPU:0, one launch (start us, length us, event | category | flops | bytes accessed | tf_op | source)
XLA Modules:
  0.0 1369.1 jit_solution(110455704509646893)
XLA Ops:
  21.0 13.2 all_gather.13
  34.2 23.2 %all-reduce.27 = f32[32]{0:T(128)S(1)} all-reduce(f32[32]{0:T(128)S(1)} %multiply_dynamic-update-slice_fusion), channel_id=2, replica_groups=mesh['dp'=8,'tensor'=4] {'dp'}, use_global_device_ids=true, to_apply=%add.27 | all-reduce | flops 32 | bytes 256
  65.6 13.4 fusion.5.x
  79.1 81.3 %narrow_forward.4 = (f32[49,16,512]{2,1,0:T(8,128)S(1)}, f32[1,512]{1,0:T(1,128)S(1)}, f32[49,16,512]{2,1,0:T(8,128)S(1)}) custom-call(f32[49,64,512]{2,1,0:T(8,128)S(1)} %fusion.5.x, f32[33]{0:T(128)S(1)} %pad_maximum_fusion.10.counts, f32[16,512]{1,0:T(8,128)S(1)} %broadcast_in_dim.79.mask, f32[1,512]{1,0:T(1,128)S(1)} %get-tuple-element.337.gain, ...), custom_call_target="tpu_custom_call" | custom-call | tf_op jit(solution)/shard_map/narrow_forward/pallas_call | solution.py:356
  167.5 4.6 collective-permute-start.1
  175.5 4.5 all-to-all-start.1
  202.6 8.3 slice_add_fusion.5
  212.9 6.2 slice_add_fusion.4
  221.0 5.7 slice_add_fusion.3
  243.5 5.6 fusion.19
  249.2 48.0 %narrow_forward.5 = (f32[49,16,512]{2,1,0:T(8,128)S(1)}, f32[1,512]{1,0:T(1,128)S(1)}, f32[49,64,512]{2,1,0:T(8,128)S(1)}) custom-call(f32[49,16,512]{2,1,0:T(8,128)S(1)} %pad_maximum_fusion.3.x, f32[33]{0:T(128)S(1)} %pad_maximum_fusion.10.counts, f32[16,512]{1,0:T(8,128)S(1)} %broadcast_in_dim.79.mask, f32[1,512]{1,0:T(1,128)S(1)} %get-tuple-element.334.gain, ...), custom_call_target="tpu_custom_call" | custom-call | tf_op jit(solution)/shard_map/narrow_forward/pallas_call | solution.py:356
  304.7 14.5 %multiply_reduce_fusion.5 = (f32[512]{0:T(512)S(1)}, f32[49,64,512]{2,1,0:T(8,128)S(1)}) fusion(f32[64]{0:T(128)S(1)} %compare_convert_fusion, f32[49,64,512]{2,1,0:T(8,128)} %copy-done.2, f32[512,512,1]{1,0,2:T(8,128)} %bitcast.77), kind=kOutput, calls=%fused_computation.29 | convolution fusion | flops 9868214272 | bytes 13895936 | tf_op jit(solution)/shard_map/dot_general | solution.py:32
  320.5 7.1 wide_exchange.4
  332.1 13.2 fusion.9.x
  345.3 49.9 %narrow_forward.6 = (f32[49,16,512]{2,1,0:T(8,128)S(1)}, f32[1,512]{1,0:T(1,128)S(1)}, f32[49,16,512]{2,1,0:T(8,128)S(1)}) custom-call(f32[49,64,512]{2,1,0:T(8,128)S(1)} %fusion.9.x, f32[33]{0:T(128)S(1)} %pad_maximum_fusion.10.counts, f32[16,512]{1,0:T(8,128)S(1)} %broadcast_in_dim.79.mask, f32[1,512]{1,0:T(1,128)S(1)} %get-tuple-element.332.gain, ...), custom_call_target="tpu_custom_call" | custom-call | tf_op jit(solution)/shard_map/narrow_forward/pallas_call | solution.py:356
  400.0 5.0 copy-done.92
  405.1 26.9 %fusion.x = f32[49,16,512]{2,1,0:T(8,128)S(1)} fusion(f32[49,16,4608]{2,1,0:T(8,128)} %copy-done.92, f32[4608,512]{1,0:T(8,128)} %all-gather.6.cloned.1.call-done), kind=kOutput, calls=%fused_computation | convolution fusion | flops 22196256768 | bytes 25493504 | tf_op jit(solution)/shard_map/dot_general | solution.py:32
  432.0 47.9 %narrow_forward.7 = (f32[49,16,512]{2,1,0:T(8,128)S(1)}, f32[1,512]{1,0:T(1,128)S(1)}, f32[49,64,512]{2,1,0:T(8,128)S(1)}) custom-call(f32[49,16,512]{2,1,0:T(8,128)S(1)} %fusion.x, f32[33]{0:T(128)S(1)} %pad_maximum_fusion.10.counts, f32[16,512]{1,0:T(8,128)S(1)} %broadcast_in_dim.79.mask, f32[1,512]{1,0:T(1,128)S(1)} %get-tuple-element.330.gain, ...), custom_call_target="tpu_custom_call" | custom-call | tf_op jit(solution)/shard_map/narrow_forward/pallas_call | solution.py:356
  483.7 14.6 %multiply_reduce_fusion.3 = (f32[512]{0:T(512)S(1)}, f32[49,64,512]{2,1,0:T(8,128)}) fusion(f32[64]{0:T(128)S(1)} %compare_convert_fusion, f32[49,64,512]{2,1,0:T(8,128)} %copy-done.3, f32[512,512,1]{1,0,2:T(8,128)S(1)} %bitcast.410), kind=kOutput, calls=%fused_computation.25 | convolution fusion | flops 9868214272 | bytes 13895936 | tf_op jit(solution)/shard_map/dot_general | solution.py:32
  498.3 4.8 reverse_bitcast_fusion
  503.1 9.6 copy.138
  516.7 7.1 wide_exchange.5
  523.9 6.1 fusion.90
  530.0 7.0 wide_exchange.6
  540.0 5.2 fusion.105.x
  545.3 49.1 %narrow_backward.4 = (f32[8,128]{1,0:T(8,128)S(1)}, f32[49,16,512]{2,1,0:T(8,128)S(1)}) custom-call(f32[49,64,512]{2,1,0:T(8,128)S(1)} %fusion.105.x, f32[33]{0:T(128)S(1)} %pad_maximum_fusion.10.counts, f32[16,512]{1,0:T(8,128)S(1)} %broadcast_in_dim.79.mask, f32[1,512]{1,0:T(1,128)S(1)} %get-tuple-element.330.gain, f32[1,512]{1,0:T(1,128)S(1)} %get-tuple-element.329.bias, ...), custom_call_target="tpu_custom_call" | custom-call | tf_op jit(solution)/shard_map/narrow_backward/pallas_call | solution.py:356
  597.6 6.6 copy-done.93
  604.2 16.9 %fusion.106.x = f32[49,16,512]{2,1,0:T(8,128)S(1)} fusion(f32[49,16,4608]{2,1,0:T(8,128)} %copy-done.93, f32[4608,512,1]{1,0,2:T(8,128)S(1)} %bitcast.409), kind=kOutput, calls=%fused_computation.397 | convolution fusion | flops 11098128384 | bytes 25493504 | tf_op jit(solution)/shard_map/dot_general | solution.py:32
  621.1 47.8 %narrow_backward.5 = (f32[8,128]{1,0:T(8,128)S(1)}, f32[49,64,512]{2,1,0:T(8,128)S(1)}) custom-call(f32[49,16,512]{2,1,0:T(8,128)S(1)} %fusion.106.x, f32[33]{0:T(128)S(1)} %pad_maximum_fusion.10.counts, f32[16,512]{1,0:T(8,128)S(1)} %broadcast_in_dim.79.mask, f32[1,512]{1,0:T(1,128)S(1)} %get-tuple-element.332.gain, f32[1,512]{1,0:T(1,128)S(1)} %get-tuple-element.331.bias, ...), custom_call_target="tpu_custom_call" | custom-call | tf_op jit(solution)/shard_map/narrow_backward/pallas_call | solution.py:356
  669.0 15.4 %fusion.89 = (f32[512]{0:T(512)S(1)}, f32[512]{0:T(512)S(1)}, f32[49,64,512]{2,1,0:T(8,128)}, f32[49,64,512]{2,1,0:T(8,128)}) fusion(f32[512]{0:T(512)S(1)} %get-tuple-element.357, f32[49,64,512]{2,1,0:T(8,128)} %copy-done.16, f32[512]{0:T(512)S(1)} %get-tuple-element.356, f32[49,64,512]{2,1,0:T(8,128)} %copy-done.20, ...), kind=kOutput, calls=%fused_computation.382 | convolution fusion | flops 4945345536 | bytes 39591936 | tf_op jit(solution)/shard_map/dot_general | solution.py:36
  684.4 7.3 wide_exchange.7
  691.7 7.2 subtract_multiply_fusion
  699.0 7.4 fusion.107.x
  706.3 48.5 %narrow_backward.6 = (f32[8,128]{1,0:T(8,128)S(1)}, f32[49,16,512]{2,1,0:T(8,128)S(1)}) custom-call(f32[49,64,512]{2,1,0:T(8,128)S(1)} %fusion.107.x, f32[33]{0:T(128)S(1)} %pad_maximum_fusion.10.counts, f32[16,512]{1,0:T(8,128)S(1)} %broadcast_in_dim.79.mask, f32[1,512]{1,0:T(1,128)S(1)} %get-tuple-element.334.gain, f32[1,512]{1,0:T(1,128)S(1)} %get-tuple-element.333.bias, ...), custom_call_target="tpu_custom_call" | custom-call | tf_op jit(solution)/shard_map/narrow_backward/pallas_call | solution.py:356
  785.4 12.9 convolution_bitcast_fusion
  800.6 7.7 fusion.109
  808.2 7.5 all-to-all-start.7
  815.8 7.7 fusion.7
  823.4 7.7 fusion.108
  846.6 4.7 collective-permute-start.5
  858.6 88.2 %narrow_backward.7 = (f32[8,128]{1,0:T(8,128)S(1)}, f32[49,64,512]{2,1,0:T(8,128)S(1)}) custom-call(f32[49,16,512]{2,1,0:T(8,128)S(1)} %multiply_add_fusion.2.x, f32[33]{0:T(128)S(1)} %pad_maximum_fusion.10.counts, f32[16,512]{1,0:T(8,128)S(1)} %broadcast_in_dim.79.mask, f32[1,512]{1,0:T(1,128)S(1)} %copy-done.15, f32[1,512]{1,0:T(1,128)S(1)} %copy-done.13, ...), custom_call_target="tpu_custom_call" | custom-call | tf_op jit(solution)/shard_map/narrow_backward/pallas_call | solution.py:356
  953.8 7.7 fusion.102
  961.6 6.7 all-to-all-done.6
  990.4 10.4 maximum_multiply_fusion
  1001.3 39.3 %psum.58 = f32[9,32]{1,0:T(8,128)} all-reduce(f32[9,32]{1,0:T(8,128)S(1)} %multiply_reduce_fusion.9), channel_id=1, replica_groups=mesh['dp'=8,'tensor'=4] {'dp','tensor'}, use_global_device_ids=true, to_apply=%region_33.34 | all-reduce | flops 288 | bytes 2304 | tf_op jit(solution)/shard_map/psum | solution.py:576
  1040.5 20.7 %bitcast_add_fusion = f32[64,49,512]{2,0,1:T(8,128)} fusion(f32[49,64,512]{2,1,0:T(8,128)} %get-tuple-element.372, f32[64,49,512]{2,0,1:T(8,128)} %param.52, f32[49,64,512]{2,1,0:T(8,128)} %get-tuple-element.371, f32[512]{0:T(512)S(1)} %copy-done.117, f32[512]{0:T(512)S(1)} %copy-done.104, f32[512]{0:T(512)S(1)} %copy-done.102, f32[512]{0:T(512)S(1)} %copy-done.108, ...), kind=kOutput, calls=%fused_computation.4 | convolution fusion | flops 4961402880 | bytes 46022912 | tf_op jit(solution)/shard_map/dot_general | solution.py:36
  1061.2 41.3 %all-reduce.32.cloned.1.call-done = f32[68,512]{1,0:T(8,128)} async-done(((f32[68,512]{1,0:T(8,128)}), f32[68,512]{1,0:T(8,128)}) %all-reduce.32.cloned.1.call-update) | async-done | bytes 139280 | tf_op jit(solution)/shard_map/psum | solution.py:576
  1105.4 246.6 %all-reduce.34.cloned.1.call-done = (f32[2048,128]{1,0:T(8,128)}, f32[1,1152,128]{2,1,0:T(8,128)}, f32[128,2048]{1,0:T(8,128)}, f32[2048,128]{1,0:T(8,128)}, f32[4608,128]{1,0:T(8,128)}, /*index=5*/f32[128,2048]{1,0:T(8,128)}) async-done(((f32[2048,128]{1,0:T(8,128)}, f32[1,1152,128]{2,1,0:T(8,128)}, f32[128,2048]{1,0:T(8,128)}, f32[2048,128]{1,0:T(8,128)}, f32[4608,128]{1,0:T(8,128)}, ...) | async-done | bytes 7143440 | tf_op jit(solution)/shard_map/psum | solution.py:572
  (614 shorter events, 202.7 us)
Async XLA Ops:
  7.2 51.1 %copy-start.82 = (f32[128,2048]{1,0:T(8,128)S(1)}, f32[128,2048]{1,0:T(8,128)}, u32[]{:S(2)}) copy-start(f32[128,2048]{1,0:T(8,128)} %param.40) | copy-start | bytes 3145732
  7.2 191.0 %all-gather.4.cloned.1.call-start = ((), (), s32[]{:S(2)}) async-start(), calls=%async_computation.10 | async-start | bytes 2949120 | tf_op jit(solution)/shard_map/all_gather | solution.py:477
  7.9 52.3 %all-to-all-start = ((f32[4,512,128]{2,1,0:T(8,128)}), f32[4,512,128]{2,1,0:T(8,128)S(1)}, u32[]{:S(2)}, u32[]{:S(2)}) async-start(f32[4,512,128]{2,1,0:T(8,128)} %bitcast.527), calls=%async_computation | async-start | bytes 2097152 | tf_op jit(solution)/shard_map/all_to_all | solution.py:460
  12.2 392.9 %all-gather.6.cloned.1.call-start = ((), (), s32[]{:S(2)}) async-start(), calls=%async_computation.11 | async-start | bytes 11796480 | tf_op jit(solution)/shard_map/all_gather | solution.py:476
  13.6 678.1 %copy-start.99 = (f32[64]{0:T(128)}, f32[64]{0:T(128)S(1)}, u32[]{:S(2)}) copy-start(f32[64]{0:T(128)S(1)} %compare_convert_fusion) | copy-start | bytes 772
  34.2 141.2 %copy-start.86 = (f32[76,512]{1,0:T(8,128)}, f32[76,512]{1,0:T(8,128)S(1)}, u32[]{:S(2)}) copy-start(f32[76,512]{1,0:T(8,128)S(1)} %all_gather.13) | copy-start | bytes 466948
  58.3 102.2 %copy-start.90 = (f32[49,32]{1,0:T(8,128)}, f32[49,32]{1,0:T(8,128)S(1)}, u32[]{:S(2)}) copy-start(f32[49,32]{1,0:T(8,128)S(1)} %copy.134) | copy-start | bytes 18820
  60.2 105.4 %copy-start.140 = (f32[16]{0:T(128)}, f32[16]{0:T(128)S(1)}, u32[]{:S(2)}) copy-start(f32[16]{0:T(128)S(1)} %slice_bitcast_fusion.23) | copy-start | bytes 196
  60.2 18.9 %copy-start.12 = (f32[1,512]{1,0:T(1,128)}, f32[1,512]{1,0:T(1,128)S(1)}, u32[]{:S(2)}) copy-start(f32[1,512]{1,0:T(1,128)S(1)} %get-tuple-element.336.bias) | copy-start | bytes 6148
  60.2 18.9 %copy-start.14 = (f32[1,512]{1,0:T(1,128)}, f32[1,512]{1,0:T(1,128)S(1)}, u32[]{:S(2)}) copy-start(f32[1,512]{1,0:T(1,128)S(1)} %get-tuple-element.337.gain) | copy-start | bytes 6148
  60.2 115.3 %all-to-all-start.2 = ((f32[4,512,128]{2,1,0:T(8,128)}), f32[4,512,128]{2,1,0:T(8,128)}, u32[]{:S(2)}, u32[]{:S(2)}) async-start(f32[4,512,128]{2,1,0:T(8,128)} %bitcast.82), calls=%async_computation.2 | async-start | bytes 2097152 | tf_op jit(solution)/shard_map/all_to_all | solution.py:460
  79.0 84.9 %copy-start.83 = (f32[128,2048]{1,0:T(8,128)S(1)}, f32[128,2048]{1,0:T(8,128)}, u32[]{:S(2)}) copy-start(f32[128,2048]{1,0:T(8,128)} %param.49) | copy-start | bytes 3145732
  162.6 3.0 collective-permute-start
  165.0 20.5 %copy-start.111 = (f32[15,32]{1,0:T(8,128)}, f32[15,32]{1,0:T(8,128)S(1)}, u32[]{:S(2)}) copy-start(f32[15,32]{1,0:T(8,128)S(1)} %slice.849) | copy-start | bytes 5764
  167.5 18.0 %collective-permute-start.1 = (f32[49,4,512]{2,1,0:T(4,128)}, f32[49,4,512]{2,1,0:T(4,128)}, u32[]{:S(2)}, u32[]{:S(2)}) collective-permute-start(f32[49,4,512]{2,1,0:T(4,128)} %get-tuple-element.236), channel_id=1, source_target_pairs={{0,1},{1,2},{2,3},{4,5},{5,6},{6,7},{8,9},{9,10},{10,11},{12,13},{... | collective-permute-start | bytes 1204232 | tf_op jit(solution)/shard_map/ppermute | solution.py:409
  172.1 13.4 collective-permute-start.2
  175.4 35.5 %copy-start.122 = (f32[128]{0:T(128)}, f32[128]{0:T(128)S(1)}, u32[]{:S(2)}) copy-start(f32[128]{0:T(128)S(1)} %get-tuple-element.344) | copy-start | bytes 1540
  175.5 35.5 %copy-start.124 = (f32[128]{0:T(128)}, f32[128]{0:T(128)S(1)}, u32[]{:S(2)}) copy-start(f32[128]{0:T(128)S(1)} %get-tuple-element.345) | copy-start | bytes 1540
  175.5 35.5 %copy-start.126 = (f32[128]{0:T(128)}, f32[128]{0:T(128)S(1)}, u32[]{:S(2)}) copy-start(f32[128]{0:T(128)S(1)} %get-tuple-element.346) | copy-start | bytes 1540
  175.5 43.7 %copy-start.128 = (f32[128]{0:T(128)}, f32[128]{0:T(128)S(1)}, u32[]{:S(2)}) copy-start(f32[128]{0:T(128)S(1)} %get-tuple-element.341) | copy-start | bytes 1540
  175.5 43.7 %copy-start.130 = (f32[128]{0:T(128)}, f32[128]{0:T(128)S(1)}, u32[]{:S(2)}) copy-start(f32[128]{0:T(128)S(1)} %get-tuple-element.342) | copy-start | bytes 1540
  175.5 43.6 %copy-start.132 = (f32[128]{0:T(128)}, f32[128]{0:T(128)S(1)}, u32[]{:S(2)}) copy-start(f32[128]{0:T(128)S(1)} %get-tuple-element.343) | copy-start | bytes 1540
  175.5 125.6 %all-to-all-start.1 = ((f32[128,4,512]{2,0,1:T(8,128)}), f32[128,4,512]{2,0,1:T(8,128)}, u32[]{:S(2)}, u32[]{:S(2)}) async-start(f32[128,4,512]{2,0,1:T(8,128)} %bitcast.448), calls=%async_computation.1 | async-start | bytes 2097152 | tf_op jit(solution)/shard_map/all_to_all | solution.py:461
  301.1 182.6 %all-to-all-start.3 = ((f32[128,4,512]{2,0,1:T(8,128)}), f32[128,4,512]{2,0,1:T(8,128)S(1)}, u32[]{:S(2)}, u32[]{:S(2)}) async-start(f32[128,4,512]{2,0,1:T(8,128)} %bitcast.447), calls=%async_computation.3 | async-start | bytes 2097152 | tf_op jit(solution)/shard_map/all_to_all | solution.py:461
  304.7 685.1 %reduce-scatter.3.cloned.1.call-start = ((), (), s32[]{:S(2)}) async-start(), calls=%async_computation.13 | async-start | bytes 2949120 | tf_op jit(solution)/shard_map/reduce_scatter | solution.py:571
  304.7 22.9 %slice-start = ((s8[6422528]{0:T(1024)(128)(4,1)}), s8[4194304]{0:T(1024)(128)(4,1)S(1)}, s32[]{:S(2)}) async-start(s8[6422528]{0:T(1024)(128)(4,1)} %bitcast.404), calls=%async_computation.16 | async-start | bytes 8388608
  304.7 22.9 %slice-start.1 = ((s8[6422528]{0:T(1024)(128)(4,1)}), s8[2228224]{0:T(1024)(128)(4,1)S(1)}, s32[]{:S(2)}) async-start(s8[6422528]{0:T(1024)(128)(4,1)} %bitcast.404), calls=%async_computation.17 | async-start | bytes 4456448
  327.6 364.1 %copy-start.94 = (f32[512]{0:T(512)}, f32[512]{0:T(512)S(1)}, u32[]{:S(2)}) copy-start(f32[512]{0:T(512)S(1)} %get-tuple-element.356) | copy-start | bytes 6148
  327.6 364.1 %copy-start.96 = (f32[512]{0:T(512)}, f32[512]{0:T(512)S(1)}, u32[]{:S(2)}) copy-start(f32[512]{0:T(512)S(1)} %get-tuple-element.357) | copy-start | bytes 6148
  604.2 64.8 %copy-start.31 = (f32[512,512,1]{1,0,2:T(8,128)S(1)}, f32[512,512,1]{1,0,2:T(8,128)}, u32[]{:S(2)}) copy-start(f32[512,512,1]{1,0,2:T(8,128)} %reshape.607) | copy-start | bytes 3145732
  691.7 66.8 %slice-start.9 = ((s8[5419008]{0:T(1024)(128)(4,1)}), s8[4194304]{0:T(1024)(128)(4,1)S(1)}, s32[]{:S(2)}) async-start(s8[5419008]{0:T(1024)(128)(4,1)} %bitcast.530), calls=%async_computation.25 | async-start | bytes 8388608
  698.9 59.6 %slice-start.10 = ((s8[5419008]{0:T(1024)(128)(4,1)}), s8[1224704]{0:T(1024)(128)(4,1)S(1)}, s32[]{:S(2)}) async-start(s8[5419008]{0:T(1024)(128)(4,1)} %bitcast.530), calls=%async_computation.26 | async-start | bytes 2449408
  755.0 4.3 collective-permute-start.3
  757.1 4.4 collective-permute-start.4
  785.4 204.4 %reduce-scatter.5.cloned.1.call-start = ((), (), s32[]{:S(2)}) async-start(), calls=%async_computation.14 | async-start | bytes 11796480 | tf_op jit(solution)/shard_map/reduce_scatter | solution.py:570
  808.2 31.7 %all-to-all-start.7 = ((f32[4,128,512]{2,1,0:T(8,128)}), f32[4,128,512]{2,1,0:T(8,128)}, u32[]{:S(2)}, u32[]{:S(2)}) async-start(f32[4,128,512]{2,1,0:T(8,128)} %bitcast.230), calls=%async_computation.9 | async-start | bytes 2097152 | tf_op jit(solution)/shard_map/all_to_all | solution.py:460
  840.0 109.5 %all-to-all-start.5 = ((f32[4,128,512]{2,1,0:T(8,128)}), f32[4,128,512]{2,1,0:T(8,128)}, u32[]{:S(2)}, u32[]{:S(2)}) async-start(f32[4,128,512]{2,1,0:T(8,128)} %bitcast.451), calls=%async_computation.6 | async-start | bytes 2097152 | tf_op jit(solution)/shard_map/all_to_all | solution.py:460
  846.6 9.0 collective-permute-start.5
  949.5 18.8 %all-to-all-start.6 = ((f32[512,4,128]{0,2,1:T(8,128)}), f32[512,4,128]{0,2,1:T(8,128)}, u32[]{:S(2)}, u32[]{:S(2)}) async-start(f32[512,4,128]{0,2,1:T(8,128)} %bitcast.450), calls=%async_computation.7 | async-start | bytes 2097152 | tf_op jit(solution)/shard_map/all_to_all | solution.py:461
  953.8 19.0 %copy-start.36 = (f32[49,23,128]{2,1,0:T(8,128)S(1)}, f32[49,23,128]{2,1,0:T(8,128)}, u32[]{:S(2)}) copy-start(f32[49,23,128]{2,1,0:T(8,128)} %copy-done.35) | copy-start | bytes 1731076
  953.8 19.0 %copy-start.38 = (f32[49,23,128]{2,1,0:T(8,128)S(1)}, f32[49,23,128]{2,1,0:T(8,128)}, u32[]{:S(2)}) copy-start(f32[49,23,128]{2,1,0:T(8,128)} %copy-done.37) | copy-start | bytes 1731076
  953.8 20.5 %copy-start.110 = (f32[16,32]{1,0:T(8,128)S(1)}, f32[16,32]{1,0:T(8,128)}, u32[]{:S(2)}) copy-start(f32[16,32]{1,0:T(8,128)} %copy-done.109) | copy-start | bytes 6148
  953.8 20.5 %copy-start.112 = (f32[15,32]{1,0:T(8,128)S(1)}, f32[15,32]{1,0:T(8,128)}, u32[]{:S(2)}) copy-start(f32[15,32]{1,0:T(8,128)} %copy-done.111) | copy-start | bytes 5764
  953.8 20.5 %copy-start.153 = (f32[1,32]{1,0:T(1,128)S(1)}, f32[1,32]{1,0:T(1,128)}, u32[]{:S(2)}) copy-start(f32[1,32]{1,0:T(1,128)} %copy-done.152) | copy-start | bytes 388
  968.3 18.9 %all-to-all-start.4 = ((f32[512,4,128]{0,2,1:T(8,128)}), f32[512,4,128]{0,2,1:T(8,128)}, u32[]{:S(2)}, u32[]{:S(2)}) async-start(f32[512,4,128]{0,2,1:T(8,128)} %bitcast.452), calls=%async_computation.4 | async-start | bytes 2097152 | tf_op jit(solution)/shard_map/all_to_all | solution.py:461
  972.7 129.8 %all-reduce.32.cloned.1.call-start = ((), (), s32[]{:S(2)}) async-start(), calls=%async_computation.12 | async-start | bytes 294912 | tf_op jit(solution)/shard_map/psum | solution.py:576
  976.6 375.4 %all-reduce.34.cloned.1.call-start = ((), (), s32[]{:S(2)}) async-start(), calls=%async_computation.15 | async-start | bytes 14286848 | tf_op jit(solution)/shard_map/psum | solution.py:572
  990.4 50.2 %copy-start.29 = (f32[512,512,1]{1,0,2:T(8,128)S(1)}, f32[512,512,1]{1,0,2:T(8,128)}, u32[]{:S(2)}) copy-start(f32[512,512,1]{1,0,2:T(8,128)} %copy-done.28) | copy-start | bytes 3145732
  (138 other events, 848.1 us)
Sparse Core Ops, SparseCore 0:
  9.6 32.0 all-gather.3
  43.2 105.6 all-gather.5
  785.5 42.8 reduce-scatter.2
  831.0 113.7 reduce-scatter.4
  980.3 122.1 all-reduce.31
  1110.1 241.8 all-reduce.33
